TPU v7x, 32 devices: a whole 2x2x4 slice. The times are simulated.
32 devices in a mesh: dp: 8 (over z, x), tensor: 4 (over y, core).
Axes of the slice: x: 2, y: 2, z: 4, core: 2. Of those that a mesh axis runs over, the one named last changes fastest.
Arguments:
- tokens: bfloat16 [64, 532, 768], P(('dp', 'tensor')), may hold values from -6 to 6
- segment_lengths: int32 [64], P(('dp', 'tensor')), may hold values from 256 to 512, as said below
- cotangent: bfloat16 [64, 532, 768], P(('dp', 'tensor')), may hold values from -6 to 6
- attention_master: float32 [3072, 768], P(('dp', 'tensor'))
- attention_mean: float32 [3072, 768], P(('dp', 'tensor')), may hold values from -32 to 32
- attention_square: float32 [3072, 768], P(('dp', 'tensor')), may hold values from 3.06432 to 12.25728
- up_master: float32 [768, 3072], P('dp', 'tensor'), may hold values from -0.21875 to 0.21875
- up_mean: float32 [768, 3072], P('dp', 'tensor'), may hold values from -32 to 32
- up_square: float32 [768, 3072], P('dp', 'tensor'), may hold values from 3.06432 to 12.25728
- down_master: float32 [768, 3072], P('dp', 'tensor'), may hold values from -0.109375 to 0.109375
- down_mean: float32 [768, 3072], P('dp', 'tensor'), may hold values from -32 to 32
- down_square: float32 [768, 3072], P('dp', 'tensor'), may hold values from 3.06432 to 12.25728
- vector_master: float32 [768, 12], P('dp')
- vector_mean: float32 [768, 12], P('dp'), may hold values from -64 to 64
- vector_square: float32 [768, 12], P('dp'), may hold values from 8.512 to 34.048
Outputs:
- block_output: bfloat16 [64, 532, 768], P(('dp', 'tensor'))
- input_grad: float32 [64, 532, 768], P(('dp', 'tensor'))
- attention_weights: float32 [3072, 768], P(('dp', 'tensor'))
- attention_first: float32 [3072, 768], P(('dp', 'tensor'))
- attention_second: float32 [3072, 768], P(('dp', 'tensor'))
- up_weights: float32 [768, 3072], P('dp', 'tensor')
- up_first: float32 [768, 3072], P('dp', 'tensor')
- up_second: float32 [768, 3072], P('dp', 'tensor')
- down_weights: float32 [768, 3072], P('dp', 'tensor')
- down_first: float32 [768, 3072], P('dp', 'tensor')
- down_second: float32 [768, 3072], P('dp', 'tensor')
- vector_params: float32 [768, 12], P('dp')
- vector_first: float32 [768, 12], P('dp')
- vector_second: float32 [768, 12], P('dp')
Inputs may be any that keep to these rules, and one draw needn't show every extreme that they name: `segment_lengths`: live token slots per segment; some segment has all 512 live.
All inputs are finite; a program needn't handle non-finite values.
Results may differ from a plain program's by a relative error of at most 0.013.
The roundings to bfloat16 on the way count: a program that leaves them out, or rounds other values in their place, can miss the bound.
Values may be sent and summed in bfloat16 or wider, within the bound.
A program may use at most 256 MiB of HBM per device.

v0:
```python
import functools

import jax
import jax.numpy as jnp
from jax import lax
from jax.experimental import pallas as pl
from jax.experimental.pallas import tpu as pltpu
from jax.sharding import PartitionSpec as P


HEAD_DIM = 64
MEM = 10
norm_epsilon = 1e-12
inv_root_two = 0.7071067811865476
inv_root_tau = 0.3989422804014327
F32, BF = jnp.float32, jnp.bfloat16
NT = (((1,), (1,)), ((), ()))
TN = (((0,), (0,)), ((), ()))
NN = (((1,), (0,)), ((), ()))

def mm(a, b, dims=NN):
    return lax.dot_general(a, b, dims, preferred_element_type=F32)

def whole(shape=None):
    return pl.BlockSpec(memory_space=pltpu.VMEM)

def norm_stats(signal, width):
    centre = signal - jnp.sum(signal, axis=-1, keepdims=True) * (1.0 / width)
    inverse = lax.rsqrt(jnp.sum(centre * centre, axis=-1, keepdims=True) * (1.0 / width) + norm_epsilon)
    return centre * inverse, inverse

def norm_back(up, scaled, inverse, width):
    return inverse * (up - jnp.sum(up, axis=-1, keepdims=True) * (1.0 / width)
                      - scaled * (jnp.sum(up * scaled, axis=-1, keepdims=True) * (1.0 / width)))

def attn_fwd_kernel(seg_rows, len_ref, x_ref, w_ref, tab_ref, q_ref, k_ref, v_ref, c_ref, n_ref, inv_ref, ab_ref, lse_ref, xs, ct):
    rows, width = xs.shape
    heads = width // HEAD_DIM
    xs[pl.ds(0, seg_rows), :] = x_ref[0]
    xs[pl.ds(seg_rows, rows - seg_rows), :] = jnp.zeros((rows - seg_rows, width), BF)
    x = xs[...]
    q_ref[0] = ((mm(x, w_ref[0]) + tab_ref[0:1, :]).astype(BF) * BF(HEAD_DIM ** -0.5)).astype(BF)
    k_ref[0] = mm(x, w_ref[1]).astype(BF)
    v_ref[0] = (mm(x, w_ref[2]) + tab_ref[1:2, :]).astype(BF)
    live = len_ref[pl.program_id(0)] + MEM
    key_at = lax.broadcasted_iota(jnp.int32, (rows, 1), 0)
    usable = (key_at < live) | ((key_at >= seg_rows - MEM) & (key_at < seg_rows))
    bias = jnp.where(usable, 0.0, -1e30).astype(F32)
    lane = lax.broadcasted_iota(jnp.int32, (rows, 2 * HEAD_DIM), 1)
    zero = jnp.zeros((), BF)

    def pair(i, carry):
        at = pl.ds(pl.multiple_of(i * 2 * HEAD_DIM, 2 * HEAD_DIM), 2 * HEAD_DIM)
        q2, k2, v2 = q_ref[0, :, at], k_ref[0, :, at], v_ref[0, :, at]
        vt = v2.T
        for h in range(2):
            mine = (lane < HEAD_DIM) if h == 0 else (lane >= HEAD_DIM)
            qh = jnp.where(mine, q2, zero)
            s = mm(k2, qh, NT) + bias
            top = jnp.max(s, axis=0, keepdims=True)
            e = jnp.exp(s - top)
            tot = jnp.sum(e, axis=0, keepdims=True)
            p = (e * (1.0 / tot)).astype(BF)
            ct[pl.ds(pl.multiple_of(i * 2 * HEAD_DIM + h * HEAD_DIM, HEAD_DIM), HEAD_DIM), :] = mm(vt[h * HEAD_DIM:(h + 1) * HEAD_DIM], p)
            lse_ref[0, pl.ds(2 * i + h, 1), :] = top + jnp.log(tot)
        return carry
    lax.fori_loop(0, heads // 2, pair, 0)
    c = ct[...].T.astype(BF)
    c_ref[0] = c
    r = x.astype(F32) + mm(c, w_ref[3]) + tab_ref[2:3, :]
    n, inv = norm_stats(r, width)
    n_ref[0] = n
    inv_ref[0] = jnp.broadcast_to(inv, (rows, 128))
    ab_ref[0] = (n * tab_ref[3:4, :] + tab_ref[4:5, :]).astype(BF)

def attn_fwd(lengths, tokens, weights, table):
    segs, seg_rows, width = tokens.shape
    rows = -(-seg_rows // 16) * 16
    heads = width // HEAD_DIM
    hp = -(-heads // 8) * 8
    seg = lambda *s: pl.BlockSpec((1,) + s, lambda i, L: (i,) + (0,) * len(s))
    full = lambda *s: pl.BlockSpec(s, lambda i, L: (0,) * len(s), pipeline_mode=pl.Buffered(1))
    sd = jax.ShapeDtypeStruct
    return pl.pallas_call(
        functools.partial(attn_fwd_kernel, seg_rows),
        grid_spec=pltpu.PrefetchScalarGridSpec(
            num_scalar_prefetch=1, grid=(segs,),
            in_specs=[seg(seg_rows, width), full(*weights.shape), full(*table.shape)],
            out_specs=[seg(rows, width)] * 5 + [seg(rows, 128), seg(rows, width), seg(hp, rows)],
            scratch_shapes=[pltpu.VMEM((rows, width), BF), pltpu.VMEM((width, rows), F32)]),
        out_shape=[sd((segs, rows, width), BF)] * 4 + [sd((segs, rows, width), F32), sd((segs, rows, 128), F32), sd((segs, rows, width), BF), sd((segs, hp, rows), F32)],
        compiler_params=pltpu.CompilerParams(vmem_limit_bytes=56 << 20),
        name="attention_forward",
    )(lengths, tokens, weights, table)

def ffn_kernel(seg_rows, block, ab_ref, n1_ref, inv_ref, cot_ref, up_ref, down_ref, tab_ref,
               out_ref, dr1_ref, dup_ref, ddown_ref, dvec_ref, hid, slope, dy, du):
    segs, rows, width = n1_ref.shape
    total = segs * rows
    chunks = up_ref.shape[0]
    per = rows // block
    nb = total // block
    def rb(i):
        return pl.ds(pl.multiple_of(i * block, block), block)
    y = dr1_ref
    def fwd(i, carry):
        a = ab_ref[rb(i), :]
        acc = jnp.zeros((block, width), F32)
        for j in range(chunks):
            u = mm(a, up_ref[j]) + tab_ref[8 + j:9 + j, :]
            phi = 0.5 * (1.0 + lax.erf(u * inv_root_two))
            h = (u * phi).astype(BF)
            hid[j, rb(i), :] = h
            slope[j, rb(i), :] = phi + u * jnp.exp(-0.5 * u * u) * inv_root_tau
            acc = acc + mm(h, down_ref[j], NT)
        y[rb(i), :] = acc
        return carry
    lax.fori_loop(0, nb, fwd, 0)
    dvec_ref[...] = jnp.zeros_like(dvec_ref)
    for s in range(segs):
        at = pl.ds(s * rows, rows)
        n1 = n1_ref[s]
        r2 = n1 * tab_ref[3:4, :] + tab_ref[4:5, :] + (y[at, :] + tab_ref[7:8, :])
        n2, inv2 = norm_stats(r2, width)
        out_ref[s] = (n2 * tab_ref[5:6, :] + tab_ref[6:7, :])[:seg_rows].astype(BF)
        live = lax.broadcasted_iota(jnp.int32, (rows, 1), 0) < seg_rows
        e = jnp.concatenate([cot_ref[s].astype(F32), jnp.zeros((rows - seg_rows, width), F32)], axis=0)
        dvec_ref[5:6, :] += jnp.sum(e * n2, axis=0, keepdims=True)
        dvec_ref[6:7, :] += jnp.sum(e, axis=0, keepdims=True)
        dr2 = norm_back(e * tab_ref[5:6, :], n2, inv2, width)
        d16 = dr2.astype(BF)
        y[at, :] = dr2
        dy[at, :] = d16
        dvec_ref[7:8, :] += jnp.sum(d16.astype(F32), axis=0, keepdims=True)
    dyt = dy[...].T
    abt = ab_ref[...].T
    for j in range(chunks):
        def back(i, carry):
            g = dy[rb(i), :]
            d = (mm(g, down_ref[j]) * slope[j, rb(i), :]).astype(BF)
            du[rb(i), :] = d
            return carry + jnp.sum(d.astype(F32), axis=0, keepdims=True)
        dvec_ref[8 + j:9 + j, :] = lax.fori_loop(0, nb, back, jnp.zeros((1, width), F32))
        ddown_ref[j] = mm(dyt, hid[j]).astype(BF)
        dup_ref[j] = mm(abt, du[...]).astype(BF)
        def inner(i, carry):
            part = mm(du[rb(i), :], up_ref[j], NT)
            slope[0, rb(i), :] = part if j == 0 else slope[0, rb(i), :] + part
            return carry
        lax.fori_loop(0, nb, inner, 0)
    for s in range(segs):
        at = pl.ds(s * rows, rows)
        da = y[at, :] + slope[0, at, :].astype(BF).astype(F32)
        n1 = n1_ref[s]
        dvec_ref[3:4, :] += jnp.sum(da * n1, axis=0, keepdims=True)
        dvec_ref[4:5, :] += jnp.sum(da, axis=0, keepdims=True)
        dr1 = norm_back(da * tab_ref[3:4, :], n1, inv_ref[s][:, 0:1], width)
        dr1_ref[at, :] = dr1
        dvec_ref[2:3, :] += jnp.sum(dr1.astype(BF).astype(F32), axis=0, keepdims=True)

def ffn(ab, n1, inv, cot, up, down, table):
    segs, rows, width = n1.shape
    seg_rows = cot.shape[1]
    total = segs * rows
    chunks = up.shape[0]
    sd = jax.ShapeDtypeStruct
    return pl.pallas_call(
        functools.partial(ffn_kernel, seg_rows, rows // 2),
        in_specs=[whole()] * 7, out_specs=[whole()] * 5,
        out_shape=[sd(cot.shape, BF), sd((total, width), F32), sd(up.shape, BF), sd(down.shape, BF), sd((16, width), F32)],
        scratch_shapes=[pltpu.VMEM((chunks, total, width), BF), pltpu.VMEM((chunks, total, width), F32), pltpu.VMEM((total, width), BF), pltpu.VMEM((total, width), BF)],
        compiler_params=pltpu.CompilerParams(vmem_limit_bytes=63 << 20),
        name="feed_forward",
    )(ab.reshape(total, width), n1, inv, cot, up, down, table)

def attn_bwd_kernel(seg_rows, len_ref, x_ref, w_ref, q_ref, k_ref, v_ref, c_ref, lse_ref, dr1_ref,
                    ig_ref, dw_ref, dvec_ref, dao, dc, dq, dk, dv, xs):
    segs, rows, width = q_ref.shape
    total = segs * rows
    heads = width // HEAD_DIM
    for s in range(segs):
        xs[pl.ds(s * rows, seg_rows), :] = x_ref[s]
        xs[pl.ds(s * rows + seg_rows, rows - seg_rows), :] = jnp.zeros((rows - seg_rows, width), BF)
    dao[...] = dr1_ref[...].astype(BF)
    dw_ref[3] = mm(c_ref[...].reshape(total, width).T, dao[...]).astype(BF)
    dc[...] = mm(dao[...], w_ref[3], NT).astype(BF)
    key_at = lax.broadcasted_iota(jnp.int32, (rows, 1), 0)
    lane = lax.broadcasted_iota(jnp.int32, (rows, 2 * HEAD_DIM), 1)
    zero = jnp.zeros((), BF)
    for s in range(segs):
        live = len_ref[s] + MEM
        usable = (key_at < live) | ((key_at >= seg_rows - MEM) & (key_at < seg_rows))
        bias = jnp.where(usable, 0.0, -1e30).astype(F32)
        at_rows = pl.ds(s * rows, rows)
        def pair(i, carry):
            at = pl.ds(pl.multiple_of(i * 2 * HEAD_DIM, 2 * HEAD_DIM), 2 * HEAD_DIM)
            q2, k2, v2 = q_ref[s, :, at], k_ref[s, :, at], v_ref[s, :, at]
            g2 = dc[at_rows, at]
            kt = k2.T
            dvp = jnp.zeros((rows, 2 * HEAD_DIM), F32)
            dkp = jnp.zeros((rows, 2 * HEAD_DIM), F32)
            dqt = []
            for h in range(2):
                mine = (lane < HEAD_DIM) if h == 0 else (lane >= HEAD_DIM)
                qh = jnp.where(mine, q2, zero)
                gh = jnp.where(mine, g2, zero)
                p = jnp.exp((mm(k2, qh, NT) + bias) - lse_ref[s, pl.ds(2 * i + h, 1), :])
                dp = mm(v2, gh, NT)
                dvp = dvp + mm(p.astype(BF), gh)
                ds = (p * (dp - jnp.sum(p * dp, axis=0, keepdims=True))).astype(BF)
                dkp = dkp + mm(ds, qh)
                dqt.append(mm(kt[h * HEAD_DIM:(h + 1) * HEAD_DIM], ds))
            dv[at_rows, at] = dvp.astype(BF)
            dk[at_rows, at] = dkp.astype(BF)
            dq[at_rows, at] = (jnp.concatenate(dqt, axis=0).T * (HEAD_DIM ** -0.5)).astype(BF)
            return carry
        lax.fori_loop(0, heads // 2, pair, 0)
    xt = xs[...].T
    dvec_ref[...] = jnp.zeros_like(dvec_ref)
    for j, g in enumerate((dq, dk, dv)):
        dw_ref[j] = mm(xt, g[...]).astype(BF)
    dvec_ref[0:1, :] = jnp.sum(dq[...].astype(F32), axis=0, keepdims=True)
    dvec_ref[1:2, :] = jnp.sum(dv[...].astype(F32), axis=0, keepdims=True)
    for s in range(segs):
        at = pl.ds(s * rows, rows)
        r = dr1_ref[at, :] + mm(dq[at, :], w_ref[0], NT) + mm(dk[at, :], w_ref[1], NT) + mm(dv[at, :], w_ref[2], NT)
        ig_ref[s] = r[:seg_rows]

def attn_bwd(lengths, tokens, weights, q, k, v, c, lse, dr1):
    segs, seg_rows, width = tokens.shape
    rows = q.shape[1]
    total = segs * rows
    sd = jax.ShapeDtypeStruct
    return pl.pallas_call(
        functools.partial(attn_bwd_kernel, seg_rows),
        in_specs=[pl.BlockSpec(memory_space=pltpu.SMEM)] + [whole()] * 8, out_specs=[whole()] * 3,
        out_shape=[sd(tokens.shape, F32), sd(weights.shape, BF), sd((16, width), F32)],
        scratch_shapes=[pltpu.VMEM((total, width), BF)] * 6,
        compiler_params=pltpu.CompilerParams(vmem_limit_bytes=63 << 20),
        name="attention_backward",
    )(lengths, tokens, weights, q, k, v, c, lse, dr1)

MESH = pl.DeviceIdType.MESH
F32, BF = jnp.float32, jnp.bfloat16
DMA = pltpu.SemaphoreType.DMA

def place():
    d, t = lax.axis_index("dp"), lax.axis_index("tensor")
    return d // 2, d % 2, t // 2, t % 2

def dev(z, x, y, c):
    return {"dp": z * 2 + x, "tensor": y * 2 + c}

def greet(z, x, y, c):
    b = pltpu.get_barrier_semaphore()
    for p in [((z + k) % 4, x, y, c) for k in (1, 2, 3)] + [(z, 1 - x, y, c), (z, x, 1 - y, c), (z, x, y, 1 - c)]:
        pl.semaphore_signal(b, inc=1, device_id=dev(*p), device_id_type=MESH)
    pl.semaphore_wait(b, 6)

def pick(ref, order, rows=None, **at):
    idx = tuple(at.get(ch, slice(None)) for ch in order)
    return ref.at[idx + ((rows,) if rows is not None else ())]

def send(src, dst, s, r, p):
    cp = pltpu.make_async_remote_copy(src, dst, s, r, device_id=dev(*p), device_id_type=MESH)
    cp.start()
    return cp

SHAPE = {"z": 4, "x": 2, "y": 2, "c": 2}

def gather_kernel(orders, half, *refs):
    nm = len(orders)
    ins, vec = refs[:nm], refs[nm]
    outs, vouts = refs[nm + 1:2 * nm + 1], refs[2 * nm + 1]
    loc, ssem, zs, xs, ys, cs, vs, vr = refs[2 * nm + 2:]
    z, x, y, c = place()
    greet(z, x, y, c)
    units = [(m, h) for m in range(nm) for h in range(2)]
    rows = lambda h: pl.ds(h * half, half)
    pend, locs, zc = [], [], {}
    for m in range(nm):
        cp = pltpu.make_async_copy(ins[m], pick(outs[m], orders[m], z=z, x=x, y=y, c=c), loc.at[m]); cp.start(); locs.append(cp)
    cp = pltpu.make_async_copy(vec, vouts.at[z, x], loc.at[nm]); cp.start(); locs.append(cp)
    vz = []
    for k in (1, 2, 3):
        cp = send(vec, vouts.at[z, x], vs.at[k - 1], vr.at[k - 1], ((z + k) % 4, x, y, c)); vz.append(cp); pend.append(cp)
    for u, (m, h) in enumerate(units):
        for k in (1, 2, 3):
            cp = send(ins[m].at[rows(h)], pick(outs[m], orders[m], rows(h), z=z, x=x, y=y, c=c), ssem.at[u, k - 1], zs.at[u, k - 1], ((z + k) % 4, x, y, c))
            zc[u, k] = cp; pend.append(cp)
    for cp in locs:
        cp.wait()
    for cp in vz:
        cp.wait_recv()
    vx = send(vouts.at[:, x], vouts.at[:, x], vs.at[3], vr.at[3], (z, 1 - x, y, c)); pend.append(vx)
    def st1(u):
        m, h = units[u]
        for k in (1, 2, 3):
            zc[u, k].wait_recv()
        src = pick(outs[m], orders[m], rows(h), x=x, y=y, c=c)
        p = (z, 1 - x, y, c) if h == 0 else (z, x, 1 - y, c)
        a = send(src, src, ssem.at[u, 3], xs.at[u], p)
        b = send(src, src, ssem.at[u, 4], cs.at[u, 0], (z, x, y, 1 - c))
        pend.extend((a, b))
        return a, b
    def st2(u, a):
        m, h = units[u]
        a.wait_recv()
        if h == 0:
            src, fresh, p = pick(outs[m], orders[m], rows(h), y=y, c=c), pick(outs[m], orders[m], rows(h), x=1 - x, y=y, c=c), (z, x, 1 - y, c)
        else:
            src, fresh, p = pick(outs[m], orders[m], rows(h), x=x, c=c), pick(outs[m], orders[m], rows(h), x=x, y=1 - y, c=c), (z, 1 - x, y, c)
        a2 = send(src, src, ssem.at[u, 5], ys.at[u], p)
        b2 = send(fresh, fresh, ssem.at[u, 6], cs.at[u, 1], (z, x, y, 1 - c))
        pend.extend((a2, b2))
        return a2, b2
    def st3(u, a2):
        m, h = units[u]
        a2.wait_recv()
        src = pick(outs[m], orders[m], rows(h), **({"y": 1 - y} if h == 0 else {"x": 1 - x}), c=c)
        b3 = send(src, src, ssem.at[u, 7], cs.at[u, 2], (z, x, y, 1 - c))
        pend.append(b3)
        return b3
    n = len(units)
    A, B, A2, B2, B3 = {}, {}, {}, {}, {}
    lag = 2
    for s in range(n + 2 * lag):
        if s < n:
            A[s], B[s] = st1(s)
        if 0 <= s - lag < n:
            A2[s - lag], B2[s - lag] = st2(s - lag, A[s - lag])
        if 0 <= s - 2 * lag < n:
            B3[s - 2 * lag] = st3(s - 2 * lag, A2[s - 2 * lag])
    vx.wait_recv()
    for u in range(n):
        for q in (B[u], B2[u], B3[u]):
            q.wait_recv()
    for cp in pend:
        cp.wait_send()

def gather(orders, shards, vec):
    nm = len(shards)
    rows, width = shards[0].shape
    nu = 2 * nm
    any_ = pl.BlockSpec(memory_space=pl.ANY)
    return pl.pallas_call(
        functools.partial(gather_kernel, orders, rows // 2),
        out_shape=[jax.ShapeDtypeStruct(tuple(SHAPE[ch] for ch in o) + (rows, width), s.dtype) for o, s in zip(orders, shards)] + [jax.ShapeDtypeStruct((4, 2) + vec.shape, vec.dtype)],
        in_specs=[any_] * (nm + 1), out_specs=[any_] * (nm + 1),
        scratch_shapes=[DMA((nm + 1,)), DMA((nu, 8)), DMA((nu, 3)), DMA((nu,)), DMA((nu,)), DMA((nu, 3)), DMA((4,)), DMA((4,))],
        compiler_params=pltpu.CompilerParams(collective_id=0, has_side_effects=True),
        name="gather_weights",
    )(*shards, vec)

def scatter_kernel(orders, half, *refs):
    nm = len(orders)
    ins, vec = refs[:nm], refs[nm]
    outs, vout = refs[nm + 1:2 * nm + 1], refs[2 * nm + 1]
    rest = refs[2 * nm + 2:]
    own, rc = rest[:nm], rest[nm:2 * nm]
    r1 = rest[2 * nm:4 * nm]
    r2, rz, vbuf, lsem, ssem, rsem, vs, vr = rest[4 * nm:]
    z, x, y, c = place()
    me = dict(z=z, x=x, y=y, c=c)
    greet(z, x, y, c)
    units = [(m, h) for m in range(nm) for h in range(2)]
    n = len(units)
    rows = lambda h: pl.ds(h * half, half)
    inner = [o.replace("c", "") for o in orders]
    pend = []
    core, xp, yp = (z, x, y, 1 - c), (z, 1 - x, y, c), (z, x, 1 - y, c)
    L, C0, C1, C2, C3 = {}, {}, {}, {}, {}
    for u, (m, h) in enumerate(units):
        C0[u] = send(pick(ins[m], orders[m], rows(h), c=1 - c), rc[m].at[h], ssem.at[u, 0], rsem.at[u, 0], core)
        L[u] = pltpu.make_async_copy(pick(ins[m], orders[m], rows(h), c=c), own[m].at[h], lsem.at[u])
        L[u].start()
        pend.append(C0[u])
    vbuf[0] = vec[...]
    V0 = send(vbuf.at[0], vbuf.at[1], vs.at[0], vr.at[0], core)

    def first(h):
        return "y" if h == 0 else "x"
    def second(h):
        return "x" if h == 0 else "y"
    def st1(u):
        m, h = units[u]
        C0[u].wait_recv()
        L[u].wait()
        o, r, dims = own[m].at[h], rc[m].at[h], inner[m]
        sh = [SHAPE[ch] for ch in dims]
        def body(i, _):
            at = (i // (sh[1] * sh[2]), (i // sh[2]) % sh[1], i % sh[2])
            o[at] = (o[at].astype(F32) + r[at].astype(F32)).astype(BF)
            return 0
        lax.fori_loop(0, sh[0] * sh[1] * sh[2], body, 0)
        f = first(h)
        C1[u] = send(pick(o, dims, **{f: 1 - me[f]}), r1[u], ssem.at[u, 1], rsem.at[u, 1], yp if h == 0 else xp)
        pend.append(C1[u])
    def st2(u):
        m, h = units[u]
        C1[u].wait_recv()
        f, s = first(h), second(h)
        o = pick(own[m].at[h], inner[m], **{f: me[f]})
        left = inner[m].replace(f, "")
        sh = [SHAPE[ch] for ch in left]
        def body(i, _):
            at = (i // sh[1], i % sh[1])
            o[at] = (o[at].astype(F32) + r1[u][at].astype(F32)).astype(BF)
            return 0
        lax.fori_loop(0, 8, body, 0)
        C2[u] = send(pick(o, left, **{s: 1 - me[s]}), r2.at[u], ssem.at[u, 2], rsem.at[u, 2], xp if h == 0 else yp)
        pend.append(C2[u])
    def st3(u):
        m, h = units[u]
        C2[u].wait_recv()
        o = pick(own[m].at[h], inner[m], x=x, y=y)
        def body(i, _):
            o[i] = (o[i].astype(F32) + r2[u, i].astype(F32)).astype(BF)
            return 0
        lax.fori_loop(0, 4, body, 0)
        for k in (1, 2, 3):
            C3[u, k] = send(o.at[(z + k) % 4], rz.at[u, k - 1], ssem.at[u, 2 + k], rsem.at[u, 2 + k], ((z + k) % 4, x, y, c))
            pend.append(C3[u, k])
    def st4(u):
        m, h = units[u]
        for k in (1, 2, 3):
            C3[u, k].wait_recv()
        o = pick(own[m].at[h], inner[m], x=x, y=y)
        outs[m][rows(h)] = ((o[z].astype(F32) + rz[u, 0].astype(F32)) + rz[u, 1].astype(F32)) + rz[u, 2].astype(F32)
    vstage = []
    def v1():
        V0.wait_recv()
        vbuf[0] = vbuf[0] + vbuf[1]
    steps = n + 3
    vq = {}
    lag = (0, 1, 2, 3)
    for s in range(n + 3):
        for k, st in enumerate((st1, st2, st3, st4)):
            u = s - k
            if 0 <= u < n:
                st(u)
        if s == 0:
            V0.wait_recv(); V0.wait_send()
            vbuf[0] = vbuf[0] + vbuf[1]
            vq["y"] = send(vbuf.at[0], vbuf.at[2], vs.at[1], vr.at[1], yp)
        if s == 1:
            vq["y"].wait_recv(); vq["y"].wait_send()
            vbuf[0] = vbuf[0] + vbuf[2]
            vq["x"] = send(vbuf.at[0], vbuf.at[3], vs.at[2], vr.at[2], xp)
        if s == 2:
            vq["x"].wait_recv(); vq["x"].wait_send()
            vbuf[4 + z] = vbuf[0] + vbuf[3]
            for k in (1, 2, 3):
                vq[k] = send(vbuf.at[4 + z], vbuf.at[4 + z], vs.at[2 + k], vr.at[2 + k], ((z + k) % 4, x, y, c))
        if s == 3:
            for k in (1, 2, 3):
                vq[k].wait_recv()
            vout[...] = ((vbuf[4] + vbuf[5]) + vbuf[6]) + vbuf[7]
            pend.extend(vq[k] for k in (1, 2, 3))
    for cp in pend:
        cp.wait_send()

def scatter(orders, grads, vec):
    nm = len(grads)
    rows, width = grads[0].shape[-2:]
    half = rows // 2
    nu = 2 * nm
    any_ = pl.BlockSpec(memory_space=pl.ANY)
    vm = pl.BlockSpec(memory_space=pltpu.VMEM)
    shp = lambda o: tuple(SHAPE[ch] for ch in o.replace("c", ""))
    st = [pltpu.VMEM((2,) + shp(o) + (half, width), BF) for o in orders]
    return pl.pallas_call(
        functools.partial(scatter_kernel, orders, half),
        out_shape=[jax.ShapeDtypeStruct((rows, width), F32)] * nm + [jax.ShapeDtypeStruct(vec.shape, F32)],
        in_specs=[any_] * nm + [vm], out_specs=[vm] * (nm + 1),
        scratch_shapes=st + st + [*[pltpu.VMEM((4, 2, half, width), BF) if (h == 0 or o == "zxyc") else pltpu.VMEM((2, 4, half, width), BF) for o in orders for h in range(2)], pltpu.VMEM((nu, 4, half, width), BF), pltpu.VMEM((nu, 3, half, width), BF), pltpu.VMEM((8,) + vec.shape, F32),
            DMA((nu,)), DMA((nu, 6)), DMA((nu, 6)), DMA((6,)), DMA((6,))],
        compiler_params=pltpu.CompilerParams(collective_id=1, has_side_effects=True, vmem_limit_bytes=56 << 20),
        name="scatter_sums",
    )(*grads, vec)


class Legs:
    def __init__(self, ssem, rsem):
        self.ssem, self.rsem, self.make, self.count = ssem, rsem, {}, 0

    def add(self, key, src, dst, peer):
        i = self.count
        self.count += 1
        self.make[key] = lambda: pltpu.make_async_remote_copy(
            src(), dst(), self.ssem.at[i], self.rsem.at[i], device_id=dev(*peer), device_id_type=MESH)

    def start(self, *keys):
        for k in keys:
            self.make[k]().start()

    def got(self, *keys):
        for k in keys:
            self.make[k]().wait_recv()

    def sent(self, *keys):
        for k in keys:
            self.make[k]().wait_send()

def add_spread(legs, key, view, place_now, h):
    z, x, y, c = place_now
    core, xp, yp = (z, x, y, 1 - c), (z, 1 - x, y, c), (z, x, 1 - y, c)
    def leg(name, peer, **at):
        legs.add((key, name), lambda: view(**at), lambda: view(**at), peer)
    leg("s1", xp if h == 0 else yp, x=x, y=y, c=c)
    leg("k1", core, x=x, y=y, c=c)
    if h == 0:
        leg("s2", yp, y=y, c=c)
        leg("k2", core, x=1 - x, y=y, c=c)
        leg("k3", core, y=1 - y, c=c)
    else:
        leg("s2", xp, x=x, c=c)
        leg("k2", core, x=x, y=1 - y, c=c)
        leg("k3", core, x=1 - x, c=c)

N_FORWARD_LEGS = 3 * 3 + 4 + 6 * 5 + 2 * 5 + 4 * 3 + 4 * 5

def forward_kernel(seg_rows, len_ref, tok, cot, am, um, dm, vp,
                   out_o, q_o, k_o, v_o, c_o, w_o, dr1_o, dup_o, ddn_o, lse_ref, dvec_ref,
                   wa, wu, wd, vec, tab, traw, craw, xs, cs, q, k, v, ct, cc, n1, inv, ab, hid, slo, dy, dyt, abt,
                   ssem, rsem, lsem):
    segs, rows, width = q_o.shape
    total = segs * rows
    heads = width // HEAD_DIM
    part = am.shape[0]
    z, x, y, c = here = place()
    peers_z = {i: ((z + i) % 4, x, y, c) for i in (1, 2, 3)}
    lt = pltpu.make_async_copy(tok, traw, lsem.at[0]); lt.start()
    lc = pltpu.make_async_copy(cot, craw, lsem.at[1]); lc.start()
    wa[z, x, y, c] = am[...].astype(BF)
    wu[y, c, z, x] = um[...].astype(BF)
    wd[y, c, z, x] = dm[...].astype(BF)
    vec[z, x] = vp[...]

    legs = Legs(ssem, rsem)
    pair_w = 2 * HEAD_DIM
    groups = width // (2 * pair_w)
    for g in range(groups):
        col = pl.ds(g * 2 * pair_w, 2 * pair_w)
        for i in (1, 2, 3):
            f = functools.partial(lambda col: wa.at[z, x, y, c, :, col], col)
            legs.add(("z", g, i), f, f, peers_z[i])
    for i in (1, 2, 3):
        legs.add(("vz", i), lambda: vec.at[z, x], lambda: vec.at[z, x], peers_z[i])
    legs.add("vx", lambda: vec.at[:, x], lambda: vec.at[:, x], (z, 1 - x, y, c))
    three = pl.ds(0, 3)
    def att_view(zz, col):
        return lambda **at: pick(wa, "zxycr", z=zz, **at).at[(Ellipsis,)] if False else wa.at[tuple([zz] + [at.get(ch, slice(None)) for ch in "xyc"] + [slice(None), col])]
    for g in range(groups):
        for h in range(2):
            add_spread(legs, ("a", g, h), att_view(three, pl.ds((2 * g + h) * pair_w, pair_w)), here, h)
    for h in range(2):
        add_spread(legs, ("o", h), att_view(3, pl.ds(h * (width // 2), width // 2)), here, h)
    half = part // 2
    for name, ref in (("u", wu), ("d", wd)):
        for h in range(2):
            rr = pl.ds(h * half, half)
            f = functools.partial(lambda ref, rr: ref.at[y, c, z, x, rr], ref, rr)
            for i in (1, 2, 3):
                legs.add((name, h, "z", i), f, f, peers_z[i])
            view = functools.partial(lambda ref, rr, **at: ref.at[tuple([at.get(ch, slice(None)) for ch in "yczx"] + [rr])], ref, rr)
            add_spread(legs, (name, h), view, here, h)

    def stage(units, n):
        for u in units:
            if n == 2:
                legs.got((u, "s1"))
                legs.start((u, "s2"), (u, "k2"))
            elif n == 3:
                legs.got((u, "s2"))
                legs.start((u, "k3"))
            elif n == 1:
                legs.start((u, "s1"), (u, "k1"))
            elif n == 4:
                legs.got((u, "k1"), (u, "k2"), (u, "k3"))
    A = lambda g: [("a", g, 0), ("a", g, 1)]
    O = [("o", 0), ("o", 1)]
    U, W = [("u", 0), ("u", 1)], [("d", 0), ("d", 1)]
    def zstart(name):
        for h in range(2):
            legs.start(*[(name, h, "z", i) for i in (1, 2, 3)])
    def zgot(name):
        for h in range(2):
            legs.got(*[(name, h, "z", i) for i in (1, 2, 3)])

    greet(*here)
    legs.start(*[("z", 0, i) for i in (1, 2, 3)])
    legs.start(*[("vz", i) for i in (1, 2, 3)])
    for g in range(1, groups):
        legs.start(*[("z", g, i) for i in (1, 2, 3)])
    lt.wait()
    for s in range(segs):
        xs[pl.ds(s * rows, seg_rows), :] = traw[s]
        xs[pl.ds(s * rows + seg_rows, rows - seg_rows), :] = jnp.zeros((rows - seg_rows, width), BF)
    legs.got(*[("z", 0, i) for i in (1, 2, 3)])
    stage(A(0), 1)
    lc.wait()
    for s in range(segs):
        cs[pl.ds(s * rows, seg_rows), :] = craw[s]
        cs[pl.ds(s * rows + seg_rows, rows - seg_rows), :] = jnp.zeros((rows - seg_rows, width), BF)
    legs.got(*[("z", 1, i) for i in (1, 2, 3)])
    stage(A(1), 1)
    stage(A(0), 2)
    legs.got(*[("vz", i) for i in (1, 2, 3)])
    legs.start("vx")
    legs.got(*[("z", 2, i) for i in (1, 2, 3)])
    stage(A(2), 1)
    zstart("u")
    stage(A(1), 2)
    stage(A(0), 3)
    legs.got("vx")
    lane_in = lax.broadcasted_iota(jnp.int32, (128, width), 0)
    lane_out = lax.broadcasted_iota(jnp.int32, (128, width), 1)
    acc = jnp.zeros((16, width), F32)
    for d in range(8):
        move = ((lane_out == lane_in + d * part) & (lane_in < part)).astype(BF)
        acc = acc + mm(vec[d // 2, d % 2], move)
    tab[...] = acc
    ticks = {
        1: lambda: (stage(A(2), 2), stage(A(1), 3)),
        2: lambda: (stage(O, 1), stage(A(2), 3)),
        3: lambda: (stage(O, 2), zgot("u"), stage(U, 1)),
        5: lambda: (stage(O, 3), stage(U, 2), zstart("d")),
        8: lambda: (zgot("d"), stage(W, 1)),
        9: lambda: stage(U, 3),
        11: lambda: stage(W, 2),
    }
    lane = lax.broadcasted_iota(jnp.int32, (rows, pair_w), 1)
    key_at = lax.broadcasted_iota(jnp.int32, (rows, 1), 0)
    zero = jnp.zeros((), BF)

    def body(it, carry):
        for n, f in ticks.items():
            pl.when(it == n)(lambda f=f: (f(), None)[1])
        for g in range(groups):
            pl.when(it == 4 * g)(lambda g=g: (stage(A(g), 4), None)[1])
        g = it // 4

        @pl.when(it % 4 == 0)
        def _():
            col = pl.ds(pl.multiple_of(g * 2 * pair_w, 2 * pair_w), 2 * pair_w)
            w3 = [wa[m, :, :, :, :, col].reshape(width, 2 * pair_w) for m in range(3)]
            xx = xs[...]
            q[:, col] = ((mm(xx, w3[0]) + tab[0:1, col]).astype(BF) * BF(HEAD_DIM ** -0.5)).astype(BF)
            k[:, col] = mm(xx, w3[1]).astype(BF)
            v[:, col] = (mm(xx, w3[2]) + tab[1:2, col]).astype(BF)

        s = (it // 2) % 2
        i = 2 * g + it % 2
        col = pl.ds(pl.multiple_of(i * pair_w, pair_w), pair_w)
        rr = pl.ds(pl.multiple_of(s * rows, 16), rows)
        live = len_ref[s] + MEM
        usable = (key_at < live) | ((key_at >= seg_rows - MEM) & (key_at < seg_rows))
        bias = jnp.where(usable, 0.0, -1e30).astype(F32)
        q2, k2, v2 = q[rr, col], k[rr, col], v[rr, col]
        vt = v2.T
        for h in range(2):
            mine = (lane < HEAD_DIM) if h == 0 else (lane >= HEAD_DIM)
            sc = mm(k2, jnp.where(mine, q2, zero), NT) + bias
            top = jnp.max(sc, axis=0, keepdims=True)
            e = jnp.exp(sc - top)
            tot = jnp.sum(e, axis=0, keepdims=True)
            p = (e * (1.0 / tot)).astype(BF)
            at = pl.ds(pl.multiple_of(i * pair_w + h * HEAD_DIM, HEAD_DIM), HEAD_DIM)
            ct[s, at, :] = mm(vt[h * HEAD_DIM:(h + 1) * HEAD_DIM], p).astype(BF)
            lse_ref[s, pl.ds(2 * i + h, 1), :] = top + jnp.log(tot)
        return carry
    lax.fori_loop(0, 4 * groups, body, 0)

    spill = [pltpu.make_async_copy(a.at[pl.ds(s * rows, rows)], o.at[s], lsem.at[2 + 2 * n + s]) for n, (a, o) in enumerate(((q, q_o), (k, k_o), (v, v_o))) for s in range(segs)]
    for cp in spill:
        cp.start()
    stage(O, 4)
    wcopy = pltpu.make_async_copy(wa, w_o, lsem.at[8]); wcopy.start()
    for s in range(segs):
        rr = pl.ds(s * rows, rows)
        cs_ = ct[s].T
        cc[rr, :] = cs_
        r = xs[rr, :].astype(F32) + mm(cs_, wa[3].reshape(width, width)) + tab[2:3, :]
        n, iv = norm_stats(r, width)
        n1[rr, :] = n
        inv[rr, :] = jnp.broadcast_to(iv, (rows, 128))
        ab[rr, :] = (n * tab[3:4, :] + tab[4:5, :]).astype(BF)
    ccopy = [pltpu.make_async_copy(cc.at[pl.ds(s * rows, rows)], c_o.at[s], lsem.at[9 + s]) for s in range(segs)]
    for cp in ccopy:
        cp.start()

    block = rows // 2
    nb = total // block
    chunks = 4
    def rb(i):
        return pl.ds(pl.multiple_of(i * block, 16), block)
    def up(j):
        return wu[j // 2, j % 2].reshape(width, width)
    def down(j):
        return wd[j // 2, j % 2].reshape(width, width)
    stage(U, 4)
    def fwd(i, carry):
        pl.when(i == 2)(lambda: (stage(W, 3), None)[1])
        a = ab[rb(i), :]
        for j in range(chunks):
            u = mm(a, up(j)) + tab[8 + j:9 + j, :]
            phi = 0.5 * (1.0 + lax.erf(u * inv_root_two))
            hid[j, rb(i), :] = (u * phi).astype(BF)
            slo[j, rb(i), :] = (phi + u * jnp.exp(-0.5 * u * u) * inv_root_tau).astype(BF)
        return carry
    lax.fori_loop(0, nb, fwd, 0)
    stage(W, 4)
    dvec_ref[...] = jnp.zeros_like(dvec_ref)
    def mid(i, carry):
        yy = tab[7:8, :]
        for j in range(chunks):
            yy = yy + mm(hid[j, rb(i), :], down(j), NT)
        nn = n1[rb(i), :]
        r2 = nn * tab[3:4, :] + tab[4:5, :] + yy
        n2, inv2 = norm_stats(r2, width)
        e = cs[rb(i), :].astype(F32)
        cs[rb(i), :] = (n2 * tab[5:6, :] + tab[6:7, :]).astype(BF)
        dvec_ref[5:6, :] += jnp.sum(e * n2, axis=0, keepdims=True)
        dvec_ref[6:7, :] += jnp.sum(e, axis=0, keepdims=True)
        dr2 = norm_back(e * tab[5:6, :], n2, inv2, width)
        g16 = dr2.astype(BF)
        dy[rb(i), :] = g16
        dvec_ref[7:8, :] += jnp.sum(g16.astype(F32), axis=0, keepdims=True)
        da = jnp.zeros((block, width), F32)
        for j in range(chunks):
            d16 = (mm(g16, down(j)) * slo[j, rb(i), :].astype(F32)).astype(BF)
            slo[j, rb(i), :] = d16
            dvec_ref[8 + j:9 + j, :] += jnp.sum(d16.astype(F32), axis=0, keepdims=True)
            da = da + mm(d16, up(j), NT)
        da = dr2 + da.astype(BF).astype(F32)
        dvec_ref[3:4, :] += jnp.sum(da * nn, axis=0, keepdims=True)
        dvec_ref[4:5, :] += jnp.sum(da, axis=0, keepdims=True)
        dr1 = norm_back(da * tab[3:4, :], nn, inv[rb(i), 0:1], width)
        n1[rb(i), :] = dr1
        dvec_ref[2:3, :] += jnp.sum(dr1.astype(BF).astype(F32), axis=0, keepdims=True)
        return carry
    lax.fori_loop(0, nb, mid, 0)
    dcopy = pltpu.make_async_copy(n1, dr1_o, lsem.at[0]); dcopy.start()
    for s in range(segs):
        craw[s] = cs[pl.ds(s * rows, seg_rows), :]
    ocopy = pltpu.make_async_copy(craw, out_o, lsem.at[1]); ocopy.start()
    dyt[...] = dy[...].T
    abt[...] = ab[...].T
    legs.sent(*legs.make)
    def grad_copies(j):
        return (pltpu.make_async_copy(wd.at[j // 2, j % 2], ddn_o.at[j // 2, j % 2], lsem.at[11 + 2 * (j % 2)]),
                pltpu.make_async_copy(wu.at[j // 2, j % 2], dup_o.at[j // 2, j % 2], lsem.at[12 + 2 * (j % 2)]))
    def grads(j, carry):
        shape = wd.shape[2:]
        @pl.when(j >= 2)
        def _():
            for cp in grad_copies(j - 2):
                cp.wait()
        wd[j // 2, j % 2] = mm(dyt[...], hid[j]).astype(BF).reshape(shape)
        wu[j // 2, j % 2] = mm(abt[...], slo[j]).astype(BF).reshape(shape)
        for cp in grad_copies(j):
            cp.start()
        return carry
    lax.fori_loop(0, chunks, grads, 0)
    for j in (2, 3):
        for cp in grad_copies(j):
            cp.wait()
    for cp in spill + [wcopy, dcopy, ocopy] + ccopy:
        cp.wait()

def forward(lengths, tokens, cotangent, att, up, down, piece):
    segs, seg_rows, width = tokens.shape
    part = att.shape[0]
    rows = -(-seg_rows // 16) * 16
    total = segs * rows
    hp = -(-(width // HEAD_DIM) // 8) * 8
    sd = jax.ShapeDtypeStruct
    any_, vm = pl.BlockSpec(memory_space=pl.ANY), whole()
    wshape, fshape = (4, 2, 2, 2, part, width), (2, 2, 4, 2, part, width)
    V = lambda *s, t=BF: pltpu.VMEM(s, t)
    return pl.pallas_call(
        functools.partial(forward_kernel, seg_rows),
        in_specs=[pl.BlockSpec(memory_space=pltpu.SMEM), any_, any_, vm, vm, vm, vm],
        out_specs=[any_] * 9 + [vm, vm],
        out_shape=[sd(cotangent.shape, BF)] + [sd((segs, rows, width), BF)] * 4 + [sd(wshape, BF), sd((total, width), F32), sd(fshape, BF), sd(fshape, BF), sd((segs, hp, rows), F32), sd((16, width), F32)],
        scratch_shapes=[V(*wshape), V(*fshape), V(*fshape), V(4, 2, 16, 128), V(16, width, t=F32), V(segs, seg_rows, width), V(segs, seg_rows, width),
                        V(total, width), V(total, width), V(total, width), V(total, width), V(total, width), V(segs, width, rows), V(total, width),
                        V(total, width, t=F32), V(total, 128, t=F32), V(total, width), V(4, total, width), V(4, total, width), V(total, width), V(width, total), V(width, total),
                        DMA((N_FORWARD_LEGS,)), DMA((N_FORWARD_LEGS,)), DMA((15,))],
        compiler_params=pltpu.CompilerParams(collective_id=0, has_side_effects=True, vmem_limit_bytes=63 << 20),
        name="forward_and_feed_forward_backward",
    )(lengths, tokens, cotangent, att, up, down, piece)

STEPS = 5
beta_first = 0.9
beta_second = 0.999
adam_epsilon = 1e-08
matrix_rate = 0.06
vector_rate = 0.2
weight_decay = 0.01
ORDERS = ("zxyc", "yczx", "yczx")


def adam(weight, moment_one, moment_two, gradient, step_rate, decay_rate):
    first_new = beta_first * moment_one + (1.0 - beta_first) * gradient
    second_new = beta_second * moment_two + (1.0 - beta_second) * gradient * gradient
    first_hat = first_new / (1.0 - beta_first**STEPS)
    second_hat = second_new / (1.0 - beta_second**STEPS)
    update = first_hat / (jnp.sqrt(second_hat) + adam_epsilon)
    return (weight - step_rate * (update + decay_rate * weight), first_new, second_new)


def shards(
    own_plan,
    tokens,
    segment_lengths,
    cotangent,
    attention_master,
    attention_mean,
    attention_square,
    up_master,
    up_mean,
    up_square,
    down_master,
    down_mean,
    down_square,
    vector_master,
    vector_mean,
    vector_square,
):
    width = tokens.shape[2]
    dp_count, tensor_count = lax.axis_size("dp"), lax.axis_size("tensor")
    part, columns = vector_master.shape
    spare = 16 - columns
    vec_low = vector_master.astype(BF).T
    if own_plan:
        piece = jnp.pad(vec_low, ((0, spare), (0, 128 - part)))
        block_output, q, k, v, c, w_all, dr1, d_up, d_down, lse, dvec_ffn = forward(
            segment_lengths, tokens, cotangent, attention_master, up_master, down_master, piece
        )
        w_all = w_all.reshape(4, width, width)
    else:
        low = [m.astype(BF) for m in (attention_master, up_master, down_master)]
        w_all = lax.all_gather(low[0], ("dp", "tensor"), axis=0, tiled=True)
        up_all, down_all = (lax.all_gather(m, ("tensor", "dp"), axis=0, tiled=True) for m in low[1:])
        rows = lax.all_gather(vec_low, "dp", axis=1, tiled=True).astype(F32)
        table = jnp.pad(rows, ((0, spare), (0, 0)))
        w_all = w_all.reshape(4, width, width)
        up_all = up_all.reshape(tensor_count, width, width)
        down_all = down_all.reshape(tensor_count, width, width)
        q, k, v, c, n1, inv, ab, lse = attn_fwd(segment_lengths, tokens, w_all, table)
        block_output, dr1, d_up, d_down, dvec_ffn = ffn(ab, n1, inv, cotangent, up_all, down_all, table)
    input_grad, d_attention, dvec_att = attn_bwd(segment_lengths, tokens, w_all, q, k, v, c, lse, dr1)
    d_vec = dvec_ffn + dvec_att

    if own_plan:
        cut = lambda g, order: g.reshape(tuple(SHAPE[ch] for ch in order) + (4 * width // (dp_count * tensor_count), width))
        grads = [cut(g, o) for g, o in zip((d_attention, d_up, d_down), ORDERS)]
        s_attention, s_up, s_down, s_vec = scatter(ORDERS, grads, d_vec)
        s_vec = lax.dynamic_slice_in_dim(s_vec, lax.axis_index("dp") * part, part, axis=1)
    else:
        flat = lambda g: g.astype(F32).reshape(-1, width)
        s_attention = lax.psum_scatter(flat(d_attention), ("dp", "tensor"), scatter_dimension=0, tiled=True)
        s_up, s_down = (lax.psum_scatter(flat(g), ("tensor", "dp"), scatter_dimension=0, tiled=True) for g in (d_up, d_down))
        s_vec = lax.psum(lax.psum_scatter(d_vec, "dp", scatter_dimension=1, tiled=True), "tensor")
    s_vec = s_vec[:columns].T

    attention_new = adam(attention_master, attention_mean, attention_square, s_attention, matrix_rate, weight_decay)
    up_new = adam(up_master, up_mean, up_square, s_up, matrix_rate, weight_decay)
    down_new = adam(down_master, down_mean, down_square, s_down, matrix_rate, weight_decay)
    vector_new = adam(vector_master, vector_mean, vector_square, s_vec, vector_rate, 0.0)
    return (block_output, input_grad, *attention_new, *up_new, *down_new, *vector_new)


def solution(mesh):
    rows, cols = P(("dp", "tensor")), P("dp", "tensor")
    own_plan = mesh.shape["dp"] == 8 and mesh.shape["tensor"] == 4
    return jax.shard_map(
        functools.partial(shards, own_plan),
        mesh=mesh,
        in_specs=(rows,) * 6 + (cols,) * 6 + (P("dp"),) * 3,
        out_specs=(rows,) * 5 + (cols,) * 6 + (P("dp"),) * 3,
        check_vma=False,
    )
```

profile of v0, /device:TPU:0, one launch (start us, length us, event | category | flops | bytes accessed | tf_op | source)
XLA Modules:
  0.0 285.7 jit_solution(4618900909632688616)
XLA Ops:
  0.6 0.0 copy-start
  0.7 2.9 %copy.29.tok.x_ref = bf16[2,532,768]{2,1,0:T(8,128)(2,1)} copy(bf16[2,532,768]{2,0,1:T(2,128)(2,1)} %param.15) | data formatting | bytes 3268608 | tf_op args[0]
  3.6 0.0 copy-done
  3.6 0.0 copy-start.13
  3.6 1.4 copy.30.cot
  5.0 0.0 copy-done.13
  5.0 0.6 pad.4.vp
  5.6 127.9 %forward_and_feed_forward_backward.1 = (bf16[2,532,768]{2,1,0:T(8,128)(2,1)}, bf16[2,544,768]{2,1,0:T(8,128)(2,1)}, bf16[2,544,768]{2,1,0:T(8,128)(2,1)}, bf16[2...) custom-call(s32[2]{0:T(128)} %len_ref.3, ...), custom_call_target="tpu_custom_call" | custom-call | tf_op jit(solution)/shard_map/forward_and_feed_forward_backward/pallas_call | solution.py:782
  133.5 3.9 %copy.32 = bf16[2,532,768]{2,0,1:T(2,128)(2,1)} copy(bf16[2,532,768]{2,1,0:T(8,128)(2,1)} %get-tuple-element.50) | data formatting | bytes 3268608
  137.3 47.2 %attention_backward.1 = (f32[2,532,768]{2,1,0:T(8,128)}, bf16[4,768,768]{2,1,0:T(8,128)(2,1)}, f32[16,768]{1,0:T(8,128)}) custom-call(s32[2]{0:T(128)} %len_ref.3, bf16[2,532,768]{2,1,0:T(8,128)(2,1)} %copy.29.tok.x_ref, bf16[4,768,768]{2,1,0:T(8,128)(2,1)} %bitcast.13, bf16[2,544,768]{2,1,0:T(8,128)(2,1)} %get-tuple-element.34.q_ref, ...), custom_call_target="tpu_custom_call" | custom-call | tf_op jit(solution)/shard_map/attention_backward/pallas_call | solution.py:234
  184.5 0.0 copy-start.11
  184.5 0.0 copy-start.12
  184.5 5.3 %copy.33 = f32[2,532,768]{2,0,1:T(2,128)} copy(f32[2,532,768]{2,1,0:T(8,128)} %get-tuple-element.51) | data formatting | bytes 6537216
  189.9 0.0 copy-done.11
  189.9 0.0 copy-done.12
  189.9 0.6 add.59.refs_3_
  190.5 0.0 copy-start.3
  190.5 0.0 copy-start.9
  190.5 0.0 copy-start.10
  190.5 89.0 %scatter_sums.1 = (f32[96,768]{1,0:T(8,128)}, f32[96,768]{1,0:T(8,128)}, f32[96,768]{1,0:T(8,128)}, f32[16,768]{1,0:T(8,128)}) custom-call(bf16[4,2,2,2,96,768]{5,4,3,2,1,0:T(8,128)(2,1)} %bitcast.12, bf16[2,2,4,2,96,768]{5,4,3,2,1,0:T(8,128)(2,1)} %get-tuple-element.42.refs_1_, bf16[2,2,4,2,96,768]{5,4,3,2,1,0:T(8,128)(2,1)} %get-tuple-element.43.refs_2_, ...), custom_call_target="tpu_custom_call" | custom-call | tf_op jit(solution)/shard_map/scatter_sums/pallas_call | solution.py:472
  279.5 0.0 copy-start.1
  279.5 0.0 copy-start.2
  279.5 0.0 copy-start.4
  279.5 0.0 copy-start.5
  279.6 0.0 copy-start.6
  279.6 0.0 copy-start.7
  279.6 0.0 copy-start.8
  279.6 0.0 copy-done.3
  279.6 0.0 copy-done.9
  279.6 0.0 copy-done.10
  279.6 2.1 multiply_subtract_fusion.2
  281.8 0.0 copy-done.1
  281.8 0.0 copy-done.2
  281.8 0.0 copy-done.4
  281.8 0.0 copy-done.5
  281.8 0.0 copy-done.6
  281.8 0.0 copy-done.7
  281.8 0.0 copy-done.8
  281.8 0.0 copy-start.14
  281.8 0.0 copy-start.15
  281.8 2.4 multiply_subtract_fusion
  284.3 0.0 copy-done.14
  284.3 0.0 copy-done.15
  284.3 1.4 multiply_subtract_fusion.3
  (1 shorter events, 0.0 us)
Async XLA Ops:
  0.6 2.9 %copy-start = (bf16[2,532,768]{2,0,1:T(2,128)(2,1)S(1)}, bf16[2,532,768]{2,0,1:T(2,128)(2,1)}, u32[]{:S(2)}) copy-start(bf16[2,532,768]{2,0,1:T(2,128)(2,1)} %param.17) | copy-start | bytes 4902916
  3.6 1.4 copy-start.13
  184.5 5.3 %copy-start.11 = (f32[16,768]{1,0:T(8,128)S(1)}, f32[16,768]{1,0:T(8,128)}, u32[]{:S(2)}) copy-start(f32[16,768]{1,0:T(8,128)} %get-tuple-element.44) | copy-start | bytes 147460
  184.5 5.3 %copy-start.12 = (f32[16,768]{1,0:T(8,128)S(1)}, f32[16,768]{1,0:T(8,128)}, u32[]{:S(2)}) copy-start(f32[16,768]{1,0:T(8,128)} %get-tuple-element.45) | copy-start | bytes 147460
  190.5 89.1 %copy-start.3 = (f32[96,768]{1,0:T(8,128)S(1)}, f32[96,768]{1,0:T(8,128)}, u32[]{:S(2)}) copy-start(f32[96,768]{1,0:T(8,128)} %am.1) | copy-start | bytes 884740
  190.5 89.1 %copy-start.9 = (f32[96,768]{1,0:T(8,128)S(1)}, f32[96,768]{1,0:T(8,128)}, u32[]{:S(2)}) copy-start(f32[96,768]{1,0:T(8,128)} %param.19) | copy-start | bytes 884740
  190.5 89.1 %copy-start.10 = (f32[96,768]{1,0:T(8,128)S(1)}, f32[96,768]{1,0:T(8,128)}, u32[]{:S(2)}) copy-start(f32[96,768]{1,0:T(8,128)} %param.20) | copy-start | bytes 884740
  279.5 2.2 copy-start.1
  279.5 2.2 copy-start.2
  279.5 2.2 copy-start.4
  279.5 2.2 copy-start.5
  279.6 2.2 copy-start.6
  279.6 2.2 copy-start.7
  279.6 2.2 copy-start.8
  281.8 2.5 copy-start.14
  281.8 2.5 copy-start.15
where the time goes:
time: 286 us
  Pallas kernels  264 us (92%)
  local copies, waits for them, and re-layouts  14.2 us (5%)
  other arithmetic  6.62 us (2%)
    pallas_call x1, Pallas kernels, forward(): pl.pallas_call(functools.partial(forward_kernel, seg_rows), in_specs=[pl....  128 us
    pallas_call x1, Pallas kernels, scatter(): pl.pallas_call(functools.partial(scatter_kernel, orders, half), out_shape...  89 us
    pallas_call x1, Pallas kernels, attn_bwd(): pl.pallas_call(functools.partial(attn_bwd_kernel, seg_rows), in_specs=[pl...  47.2 us
    unnamed x36, local copies, waits for them, and re-layouts  13.6 us
    sub x3, other arithmetic, adam(): weight - step_rate * (update + decay_rate * weight)  5.99 us

commit v1 on v0

--- a/solution.py
+++ b/solution.py
@@ -267,217 +267,6 @@
     return cp
 
 SHAPE = {"z": 4, "x": 2, "y": 2, "c": 2}
-
-def gather_kernel(orders, half, *refs):
-    nm = len(orders)
-    ins, vec = refs[:nm], refs[nm]
-    outs, vouts = refs[nm + 1:2 * nm + 1], refs[2 * nm + 1]
-    loc, ssem, zs, xs, ys, cs, vs, vr = refs[2 * nm + 2:]
-    z, x, y, c = place()
-    greet(z, x, y, c)
-    units = [(m, h) for m in range(nm) for h in range(2)]
-    rows = lambda h: pl.ds(h * half, half)
-    pend, locs, zc = [], [], {}
-    for m in range(nm):
-        cp = pltpu.make_async_copy(ins[m], pick(outs[m], orders[m], z=z, x=x, y=y, c=c), loc.at[m]); cp.start(); locs.append(cp)
-    cp = pltpu.make_async_copy(vec, vouts.at[z, x], loc.at[nm]); cp.start(); locs.append(cp)
-    vz = []
-    for k in (1, 2, 3):
-        cp = send(vec, vouts.at[z, x], vs.at[k - 1], vr.at[k - 1], ((z + k) % 4, x, y, c)); vz.append(cp); pend.append(cp)
-    for u, (m, h) in enumerate(units):
-        for k in (1, 2, 3):
-            cp = send(ins[m].at[rows(h)], pick(outs[m], orders[m], rows(h), z=z, x=x, y=y, c=c), ssem.at[u, k - 1], zs.at[u, k - 1], ((z + k) % 4, x, y, c))
-            zc[u, k] = cp; pend.append(cp)
-    for cp in locs:
-        cp.wait()
-    for cp in vz:
-        cp.wait_recv()
-    vx = send(vouts.at[:, x], vouts.at[:, x], vs.at[3], vr.at[3], (z, 1 - x, y, c)); pend.append(vx)
-    def st1(u):
-        m, h = units[u]
-        for k in (1, 2, 3):
-            zc[u, k].wait_recv()
-        src = pick(outs[m], orders[m], rows(h), x=x, y=y, c=c)
-        p = (z, 1 - x, y, c) if h == 0 else (z, x, 1 - y, c)
-        a = send(src, src, ssem.at[u, 3], xs.at[u], p)
-        b = send(src, src, ssem.at[u, 4], cs.at[u, 0], (z, x, y, 1 - c))
-        pend.extend((a, b))
-        return a, b
-    def st2(u, a):
-        m, h = units[u]
-        a.wait_recv()
-        if h == 0:
-            src, fresh, p = pick(outs[m], orders[m], rows(h), y=y, c=c), pick(outs[m], orders[m], rows(h), x=1 - x, y=y, c=c), (z, x, 1 - y, c)
-        else:
-            src, fresh, p = pick(outs[m], orders[m], rows(h), x=x, c=c), pick(outs[m], orders[m], rows(h), x=x, y=1 - y, c=c), (z, 1 - x, y, c)
-        a2 = send(src, src, ssem.at[u, 5], ys.at[u], p)
-        b2 = send(fresh, fresh, ssem.at[u, 6], cs.at[u, 1], (z, x, y, 1 - c))
-        pend.extend((a2, b2))
-        return a2, b2
-    def st3(u, a2):
-        m, h = units[u]
-        a2.wait_recv()
-        src = pick(outs[m], orders[m], rows(h), **({"y": 1 - y} if h == 0 else {"x": 1 - x}), c=c)
-        b3 = send(src, src, ssem.at[u, 7], cs.at[u, 2], (z, x, y, 1 - c))
-        pend.append(b3)
-        return b3
-    n = len(units)
-    A, B, A2, B2, B3 = {}, {}, {}, {}, {}
-    lag = 2
-    for s in range(n + 2 * lag):
-        if s < n:
-            A[s], B[s] = st1(s)
-        if 0 <= s - lag < n:
-            A2[s - lag], B2[s - lag] = st2(s - lag, A[s - lag])
-        if 0 <= s - 2 * lag < n:
-            B3[s - 2 * lag] = st3(s - 2 * lag, A2[s - 2 * lag])
-    vx.wait_recv()
-    for u in range(n):
-        for q in (B[u], B2[u], B3[u]):
-            q.wait_recv()
-    for cp in pend:
-        cp.wait_send()
-
-def gather(orders, shards, vec):
-    nm = len(shards)
-    rows, width = shards[0].shape
-    nu = 2 * nm
-    any_ = pl.BlockSpec(memory_space=pl.ANY)
-    return pl.pallas_call(
-        functools.partial(gather_kernel, orders, rows // 2),
-        out_shape=[jax.ShapeDtypeStruct(tuple(SHAPE[ch] for ch in o) + (rows, width), s.dtype) for o, s in zip(orders, shards)] + [jax.ShapeDtypeStruct((4, 2) + vec.shape, vec.dtype)],
-        in_specs=[any_] * (nm + 1), out_specs=[any_] * (nm + 1),
-        scratch_shapes=[DMA((nm + 1,)), DMA((nu, 8)), DMA((nu, 3)), DMA((nu,)), DMA((nu,)), DMA((nu, 3)), DMA((4,)), DMA((4,))],
-        compiler_params=pltpu.CompilerParams(collective_id=0, has_side_effects=True),
-        name="gather_weights",
-    )(*shards, vec)
-
-def scatter_kernel(orders, half, *refs):
-    nm = len(orders)
-    ins, vec = refs[:nm], refs[nm]
-    outs, vout = refs[nm + 1:2 * nm + 1], refs[2 * nm + 1]
-    rest = refs[2 * nm + 2:]
-    own, rc = rest[:nm], rest[nm:2 * nm]
-    r1 = rest[2 * nm:4 * nm]
-    r2, rz, vbuf, lsem, ssem, rsem, vs, vr = rest[4 * nm:]
-    z, x, y, c = place()
-    me = dict(z=z, x=x, y=y, c=c)
-    greet(z, x, y, c)
-    units = [(m, h) for m in range(nm) for h in range(2)]
-    n = len(units)
-    rows = lambda h: pl.ds(h * half, half)
-    inner = [o.replace("c", "") for o in orders]
-    pend = []
-    core, xp, yp = (z, x, y, 1 - c), (z, 1 - x, y, c), (z, x, 1 - y, c)
-    L, C0, C1, C2, C3 = {}, {}, {}, {}, {}
-    for u, (m, h) in enumerate(units):
-        C0[u] = send(pick(ins[m], orders[m], rows(h), c=1 - c), rc[m].at[h], ssem.at[u, 0], rsem.at[u, 0], core)
-        L[u] = pltpu.make_async_copy(pick(ins[m], orders[m], rows(h), c=c), own[m].at[h], lsem.at[u])
-        L[u].start()
-        pend.append(C0[u])
-    vbuf[0] = vec[...]
-    V0 = send(vbuf.at[0], vbuf.at[1], vs.at[0], vr.at[0], core)
-
-    def first(h):
-        return "y" if h == 0 else "x"
-    def second(h):
-        return "x" if h == 0 else "y"
-    def st1(u):
-        m, h = units[u]
-        C0[u].wait_recv()
-        L[u].wait()
-        o, r, dims = own[m].at[h], rc[m].at[h], inner[m]
-        sh = [SHAPE[ch] for ch in dims]
-        def body(i, _):
-            at = (i // (sh[1] * sh[2]), (i // sh[2]) % sh[1], i % sh[2])
-            o[at] = (o[at].astype(F32) + r[at].astype(F32)).astype(BF)
-            return 0
-        lax.fori_loop(0, sh[0] * sh[1] * sh[2], body, 0)
-        f = first(h)
-        C1[u] = send(pick(o, dims, **{f: 1 - me[f]}), r1[u], ssem.at[u, 1], rsem.at[u, 1], yp if h == 0 else xp)
-        pend.append(C1[u])
-    def st2(u):
-        m, h = units[u]
-        C1[u].wait_recv()
-        f, s = first(h), second(h)
-        o = pick(own[m].at[h], inner[m], **{f: me[f]})
-        left = inner[m].replace(f, "")
-        sh = [SHAPE[ch] for ch in left]
-        def body(i, _):
-            at = (i // sh[1], i % sh[1])
-            o[at] = (o[at].astype(F32) + r1[u][at].astype(F32)).astype(BF)
-            return 0
-        lax.fori_loop(0, 8, body, 0)
-        C2[u] = send(pick(o, left, **{s: 1 - me[s]}), r2.at[u], ssem.at[u, 2], rsem.at[u, 2], xp if h == 0 else yp)
-        pend.append(C2[u])
-    def st3(u):
-        m, h = units[u]
-        C2[u].wait_recv()
-        o = pick(own[m].at[h], inner[m], x=x, y=y)
-        def body(i, _):
-            o[i] = (o[i].astype(F32) + r2[u, i].astype(F32)).astype(BF)
-            return 0
-        lax.fori_loop(0, 4, body, 0)
-        for k in (1, 2, 3):
-            C3[u, k] = send(o.at[(z + k) % 4], rz.at[u, k - 1], ssem.at[u, 2 + k], rsem.at[u, 2 + k], ((z + k) % 4, x, y, c))
-            pend.append(C3[u, k])
-    def st4(u):
-        m, h = units[u]
-        for k in (1, 2, 3):
-            C3[u, k].wait_recv()
-        o = pick(own[m].at[h], inner[m], x=x, y=y)
-        outs[m][rows(h)] = ((o[z].astype(F32) + rz[u, 0].astype(F32)) + rz[u, 1].astype(F32)) + rz[u, 2].astype(F32)
-    vstage = []
-    def v1():
-        V0.wait_recv()
-        vbuf[0] = vbuf[0] + vbuf[1]
-    steps = n + 3
-    vq = {}
-    lag = (0, 1, 2, 3)
-    for s in range(n + 3):
-        for k, st in enumerate((st1, st2, st3, st4)):
-            u = s - k
-            if 0 <= u < n:
-                st(u)
-        if s == 0:
-            V0.wait_recv(); V0.wait_send()
-            vbuf[0] = vbuf[0] + vbuf[1]
-            vq["y"] = send(vbuf.at[0], vbuf.at[2], vs.at[1], vr.at[1], yp)
-        if s == 1:
-            vq["y"].wait_recv(); vq["y"].wait_send()
-            vbuf[0] = vbuf[0] + vbuf[2]
-            vq["x"] = send(vbuf.at[0], vbuf.at[3], vs.at[2], vr.at[2], xp)
-        if s == 2:
-            vq["x"].wait_recv(); vq["x"].wait_send()
-            vbuf[4 + z] = vbuf[0] + vbuf[3]
-            for k in (1, 2, 3):
-                vq[k] = send(vbuf.at[4 + z], vbuf.at[4 + z], vs.at[2 + k], vr.at[2 + k], ((z + k) % 4, x, y, c))
-        if s == 3:
-            for k in (1, 2, 3):
-                vq[k].wait_recv()
-            vout[...] = ((vbuf[4] + vbuf[5]) + vbuf[6]) + vbuf[7]
-            pend.extend(vq[k] for k in (1, 2, 3))
-    for cp in pend:
-        cp.wait_send()
-
-def scatter(orders, grads, vec):
-    nm = len(grads)
-    rows, width = grads[0].shape[-2:]
-    half = rows // 2
-    nu = 2 * nm
-    any_ = pl.BlockSpec(memory_space=pl.ANY)
-    vm = pl.BlockSpec(memory_space=pltpu.VMEM)
-    shp = lambda o: tuple(SHAPE[ch] for ch in o.replace("c", ""))
-    st = [pltpu.VMEM((2,) + shp(o) + (half, width), BF) for o in orders]
-    return pl.pallas_call(
-        functools.partial(scatter_kernel, orders, half),
-        out_shape=[jax.ShapeDtypeStruct((rows, width), F32)] * nm + [jax.ShapeDtypeStruct(vec.shape, F32)],
-        in_specs=[any_] * nm + [vm], out_specs=[vm] * (nm + 1),
-        scratch_shapes=st + st + [*[pltpu.VMEM((4, 2, half, width), BF) if (h == 0 or o == "zxyc") else pltpu.VMEM((2, 4, half, width), BF) for o in orders for h in range(2)], pltpu.VMEM((nu, 4, half, width), BF), pltpu.VMEM((nu, 3, half, width), BF), pltpu.VMEM((8,) + vec.shape, F32),
-            DMA((nu,)), DMA((nu, 6)), DMA((nu, 6)), DMA((6,)), DMA((6,))],
-        compiler_params=pltpu.CompilerParams(collective_id=1, has_side_effects=True, vmem_limit_bytes=56 << 20),
-        name="scatter_sums",
-    )(*grads, vec)
 
 
 class Legs:
@@ -792,6 +581,325 @@
         name="forward_and_feed_forward_backward",
     )(lengths, tokens, cotangent, att, up, down, piece)
 
+N_BACK_LEGS = 4 * 6 + 2 * 6 + 6 * 6 + 6
+
+
+def backward_kernel(seg_rows, len_ref, tok, w_i, q_i, k_i, v_i, c_i, dr1_i, dup, ddn, lse_ref, dvec_in,
+                    ig_o, ga_ref, gu_ref, gd_ref, gv_ref,
+                    wa, q, k, v, cc, r1f, traw, xs, xt, dao, own_u, own_d, rc_u, rc_d, h1_u0, h1_u1, h1_d0, h1_d1, h2_f, rz_f, rc_a, h1_a, h2_a, rz_a, rc_o, h1_o, h2_o, rz_o, vbuf,
+                    ssem, rsem, lsem):
+    segs, rows, width = q_i.shape
+    total = segs * rows
+    heads = width // HEAD_DIM
+    pair_w = 2 * HEAD_DIM
+    groups = width // (2 * pair_w)
+    part = ga_ref.shape[0]
+    half = part // 2
+    z, x, y, c = here = place()
+    me = dict(z=z, x=x, y=y, c=c)
+    core, xp, yp = (z, x, y, 1 - c), (z, 1 - x, y, c), (z, x, 1 - y, c)
+    zp = {i: ((z + i) % 4, x, y, c) for i in (1, 2, 3)}
+    h1_u, h1_d = (h1_u0, h1_u1), (h1_d0, h1_d1)
+    legs = Legs(ssem, rsem)
+    first, second = {0: "y", 1: "x"}, {0: "x", 1: "y"}
+    peer = {"x": xp, "y": yp}
+
+    load = {}
+    def local(name, src, dst, i):
+        load[name] = pltpu.make_async_copy(src, dst, lsem.at[i])
+        load[name].start()
+    local("dr1", dr1_i, r1f, 0)
+    local("w", w_i, wa, 1)
+    for s in range(segs):
+        rr = pl.ds(s * rows, rows)
+        local(("c", s), c_i.at[s], cc.at[rr], 2 + s)
+        local(("v", s), v_i.at[s], v.at[rr], 4 + s)
+        local(("k", s), k_i.at[s], k.at[rr], 6 + s)
+        local(("q", s), q_i.at[s], q.at[rr], 8 + s)
+    local("t", tok, traw, 10)
+
+    ff = [("u", dup, own_u, rc_u, h1_u), ("d", ddn, own_d, rc_d, h1_d)]
+    hop = {}
+    for n, (name, g, own, rc, h1) in enumerate(ff):
+        for h in range(2):
+            rr = pl.ds(h * half, half)
+            u = 2 * n + h
+            f, s = first[h], second[h]
+            o = own.at[h]
+            legs.add((name, h, 0), functools.partial(lambda g, rr: g.at[:, 1 - c, :, :, rr], g, rr), functools.partial(lambda rc, h: rc.at[h], rc, h), core)
+            local((name, h), g.at[:, c, :, :, rr], o, 11 + u)
+            legs.add((name, h, 1), functools.partial(lambda o, f: pick(o, "yzx", **{f: 1 - me[f]}), o, f), functools.partial(lambda h1, h: h1[h], h1, h), peer[f])
+            legs.add((name, h, 2), functools.partial(lambda o, f, s: pick(o, "yzx", **{f: me[f], s: 1 - me[s]}), o, f, s), functools.partial(lambda u: h2_f.at[u], u), peer[s])
+            for i in (1, 2, 3):
+                legs.add((name, h, 2 + i), functools.partial(lambda o, i: o.at[y, (z + i) % 4, x], o, i), functools.partial(lambda u, i: rz_f.at[u, i - 1], u, i), zp[i])
+
+    def ff_stage(name, h, n):
+        own, rc, h1 = (own_u, rc_u, h1_u) if name == "u" else (own_d, rc_d, h1_d)
+        u = 2 * (name == "d") + h
+        o, f, s = own.at[h], first[h], second[h]
+        if n == 0:
+            legs.got((name, h, 0))
+            load[name, h].wait()
+            def body(i, _):
+                at = (i // 8, (i // 2) % 4, i % 2)
+                o[at] = (o[at].astype(F32) + rc[(h,) + at].astype(F32)).astype(BF)
+                return 0
+            lax.fori_loop(0, 16, body, 0)
+            legs.start((name, h, 1))
+        elif n == 1:
+            legs.got((name, h, 1))
+            left = "yzx".replace(f, "")
+            sh = [SHAPE[ch] for ch in left]
+            o = pick(o, "yzx", **{f: me[f]})
+            def body(i, _):
+                at = (i // sh[1], i % sh[1])
+                o[at] = (o[at].astype(F32) + h1[h][at].astype(F32)).astype(BF)
+                return 0
+            lax.fori_loop(0, 8, body, 0)
+            legs.start((name, h, 2))
+        elif n == 2:
+            legs.got((name, h, 2))
+            def body(i, _):
+                o[y, i, x] = (o[y, i, x].astype(F32) + h2_f[u, i].astype(F32)).astype(BF)
+                return 0
+            lax.fori_loop(0, 4, body, 0)
+            legs.start(*[(name, h, 2 + i) for i in (1, 2, 3)])
+        else:
+            legs.got(*[(name, h, 2 + i) for i in (1, 2, 3)])
+            out = gu_ref if name == "u" else gd_ref
+            out[pl.ds(h * half, half)] = ((o[y, z, x].astype(F32) + rz_f[u, 0].astype(F32)) + rz_f[u, 1].astype(F32)) + rz_f[u, 2].astype(F32)
+
+    three = pl.ds(0, 3)
+    def att(zz, col, **at):
+        return wa.at[tuple([zz] + [at.get(ch, slice(None)) for ch in "xyc"] + [slice(None), col])]
+    def add_att(key, zz, col, rc, h1, h2, rz, h):
+        f, s = first[h], second[h]
+        legs.add((key, 0), lambda: att(zz, col, c=1 - c), lambda: rc, core)
+        legs.add((key, 1), lambda: att(zz, col, c=c, **{f: 1 - me[f]}), lambda: h1, peer[f])
+        legs.add((key, 2), lambda: att(zz, col, c=c, **{f: me[f], s: 1 - me[s]}), lambda: h2, peer[s])
+        for i in (1, 2, 3):
+            legs.add((key, 2 + i), functools.partial(lambda i: att((z + i) % 4, col, c=c, x=x, y=y), i), functools.partial(lambda i: rz.at[i - 1], i), zp[i])
+    units = {}
+    for g in range(groups):
+        for h in range(2):
+            u = 2 * g + h
+            col = pl.ds(u * pair_w, pair_w)
+            units["a", g, h] = (range(3), col, rc_a.at[u], h1_a.at[u], h2_a.at[u], rz_a.at[u], h)
+            add_att(("a", g, h), three, col, *units["a", g, h][2:])
+    for h in range(2):
+        col = pl.ds(h * (width // 2), width // 2)
+        units["o", h] = ((3,), col, rc_o.at[h], h1_o.at[h], h2_o.at[h], rz_o.at[h], h)
+        add_att(("o", h), 3, col, *units["o", h][2:])
+
+    def att_stage(key, n):
+        zs, col, rc, h1, h2, rz, h = units[key]
+        f, s = first[h], second[h]
+        one = len(zs) == 1
+        base = zs[0]
+        def sub(ref, i, *rest):
+            at = tuple(rest) if one else (i,) + tuple(rest)
+            return ref[at] if at else ref[...]
+        if n == 0:
+            legs.start((key, 0))
+            return
+        if n == 1:
+            legs.got((key, 0))
+            def body(i, _):
+                m, a, b = base + i // 4, (i // 2) % 2, i % 2
+                t = (m, a, b, c, slice(None), col)
+                wa[t] = (wa[t].astype(F32) + sub(rc, i // 4, a, b).astype(F32)).astype(BF)
+                return 0
+            lax.fori_loop(0, 4 * len(zs), body, 0)
+            legs.start((key, 1))
+        elif n == 2:
+            legs.got((key, 1))
+            def body(i, _):
+                m, a = base + i // 2, i % 2
+                t = (m, a, y, c, slice(None), col) if f == "y" else (m, x, a, c, slice(None), col)
+                wa[t] = (wa[t].astype(F32) + sub(h1, i // 2, a).astype(F32)).astype(BF)
+                return 0
+            lax.fori_loop(0, 2 * len(zs), body, 0)
+            legs.start((key, 2))
+        elif n == 3:
+            legs.got((key, 2))
+            def body(i, _):
+                t = (base + i, x, y, c, slice(None), col)
+                wa[t] = (wa[t].astype(F32) + sub(h2, i).astype(F32)).astype(BF)
+                return 0
+            lax.fori_loop(0, len(zs), body, 0)
+            for i in (1, 2, 3):
+                to = (z + i) % 4
+                pl.when((to == 3) if one else (to < 3))(functools.partial(lambda i: (legs.start((key, 2 + i)), None)[1], i))
+        else:
+            @pl.when((z == 3) if one else (z < 3))
+            def _():
+                legs.got(*[(key, 2 + i) for i in (1, 2, 3)])
+                ga_ref[:, col] = ((wa[z, x, y, c, :, col].astype(F32) + rz[0].astype(F32)) + rz[1].astype(F32)) + rz[2].astype(F32)
+
+    def att_sent(key):
+        one = key[0] == "o"
+        legs.sent((key, 0), (key, 1), (key, 2))
+        for i in (1, 2, 3):
+            to = (z + i) % 4
+            pl.when((to == 3) if one else (to < 3))(functools.partial(lambda i: (legs.sent((key, 2 + i)), None)[1], i))
+
+    legs.add("v0", lambda: vbuf.at[0], lambda: vbuf.at[1], core)
+    legs.add("v1", lambda: vbuf.at[2], lambda: vbuf.at[3], yp)
+    legs.add("v2", lambda: vbuf.at[4], lambda: vbuf.at[5], xp)
+    for i in (1, 2, 3):
+        legs.add(("v3", i), lambda: vbuf.at[6 + z], lambda: vbuf.at[6 + z], zp[i])
+
+    greet(*here)
+    for h in range(2):
+        for name in ("u", "d"):
+            legs.start((name, h, 0))
+    load["dr1"].wait()
+    dao[...] = r1f[...].astype(BF)
+    for s in range(segs):
+        load["c", s].wait()
+    load["w"].wait()
+    dwo = mm(cc[...].T, dao[...]).astype(BF)
+    dc = mm(dao[...], wa[3].reshape(width, width), NT).astype(BF)
+    cc[...] = dc
+    wa[3] = dwo.reshape(wa.shape[1:])
+    for h in range(2):
+        att_stage(("o", h), 0)
+    ff_stage("u", 0, 0)
+    ff_stage("u", 1, 0)
+    load["t"].wait()
+    for s in range(segs):
+        xs[pl.ds(s * rows, seg_rows), :] = traw[s]
+        xs[pl.ds(s * rows + seg_rows, rows - seg_rows), :] = jnp.zeros((rows - seg_rows, width), BF)
+    xt[...] = xs[...].T
+    for s in range(segs):
+        for n in "qkv":
+            load[n, s].wait()
+    vbuf[0] = dvec_in[...]
+
+    def ffs(*what):
+        return lambda: [ff_stage(*w) for w in what]
+    def atts(*what):
+        return lambda: [att_stage(*w) for w in what]
+    ticks = {
+        1: ffs(("u", 0, 1), ("u", 1, 1), ("d", 0, 0), ("d", 1, 0)),
+        3: ffs(("u", 0, 2), ("u", 1, 2)),
+        4: ffs(("d", 0, 1), ("d", 1, 1)),
+        5: ffs(("u", 0, 3), ("u", 1, 3)),
+        6: atts((("o", 0), 1), (("o", 1), 1)),
+        7: ffs(("d", 0, 2), ("d", 1, 2)),
+        8: atts((("o", 0), 2), (("o", 1), 2), (("a", 0, 0), 1), (("a", 0, 1), 1)),
+        9: ffs(("d", 0, 3), ("d", 1, 3)),
+        10: atts((("o", 0), 3), (("o", 1), 3), (("a", 0, 0), 2), (("a", 0, 1), 2)),
+        11: atts((("a", 0, 0), 3), (("a", 0, 1), 3), (("a", 1, 0), 1), (("a", 1, 1), 1)),
+    }
+    lane = lax.broadcasted_iota(jnp.int32, (rows, pair_w), 1)
+    key_at = lax.broadcasted_iota(jnp.int32, (rows, 1), 0)
+    zero = jnp.zeros((), BF)
+
+    def body(it, carry):
+        for n, f in ticks.items():
+            pl.when(it == n)(lambda f=f: (f(), None)[1])
+        g = it // 4
+        s = (it // 2) % 2
+        i = 2 * g + it % 2
+        col = pl.ds(pl.multiple_of(i * pair_w, pair_w), pair_w)
+        rr = pl.ds(pl.multiple_of(s * rows, 16), rows)
+        live = len_ref[s] + MEM
+        usable = (key_at < live) | ((key_at >= seg_rows - MEM) & (key_at < seg_rows))
+        bias = jnp.where(usable, 0.0, -1e30).astype(F32)
+        q2, k2, v2, g2 = q[rr, col], k[rr, col], v[rr, col], cc[rr, col]
+        kt = k2.T
+        dvp = jnp.zeros((rows, pair_w), F32)
+        dkp = jnp.zeros((rows, pair_w), F32)
+        dqt = []
+        for h in range(2):
+            mine = (lane < HEAD_DIM) if h == 0 else (lane >= HEAD_DIM)
+            qh = jnp.where(mine, q2, zero)
+            gh = jnp.where(mine, g2, zero)
+            p = jnp.exp((mm(k2, qh, NT) + bias) - lse_ref[s, pl.ds(2 * i + h, 1), :])
+            dp = mm(v2, gh, NT)
+            dvp = dvp + mm(p.astype(BF), gh)
+            ds = (p * (dp - jnp.sum(p * dp, axis=0, keepdims=True))).astype(BF)
+            dkp = dkp + mm(ds, qh)
+            dqt.append(mm(kt[h * HEAD_DIM:(h + 1) * HEAD_DIM], ds))
+        v[rr, col] = dvp.astype(BF)
+        k[rr, col] = dkp.astype(BF)
+        q[rr, col] = (jnp.concatenate(dqt, axis=0).T * (HEAD_DIM ** -0.5)).astype(BF)
+
+        @pl.when(it % 4 == 3)
+        def _():
+            gcol = pl.ds(pl.multiple_of(g * 2 * pair_w, 2 * pair_w), 2 * pair_w)
+            for m, ref in enumerate((q, k, v)):
+                d = ref[:, gcol]
+                r1f[...] += mm(d, wa[m, :, :, :, :, gcol].reshape(width, 2 * pair_w), NT)
+                wa[m, :, :, :, :, gcol] = mm(xt[...], d).astype(BF).reshape(2, 2, 2, part, 2 * pair_w)
+            for gg in range(groups):
+                pl.when(g == gg)(functools.partial(lambda gg: ([att_stage(("a", gg, h), 0) for h in range(2)], None)[1], gg))
+        return carry
+    lax.fori_loop(0, 4 * groups, body, 0)
+
+    vbuf[0, 0:1, :] = jnp.sum(q[...].astype(F32), axis=0, keepdims=True)
+    vbuf[0, 1:2, :] = jnp.sum(v[...].astype(F32), axis=0, keepdims=True)
+    legs.start("v0")
+    def a_all(g, n):
+        for h in range(2):
+            att_stage(("a", g, h), n)
+    a_all(1, 2)
+    a_all(2, 1)
+    legs.got("v0")
+    vbuf[2] = vbuf[0] + vbuf[1]
+    legs.start("v1")
+    for h in range(2):
+        att_stage(("o", h), 4)
+    a_all(1, 3)
+    a_all(2, 2)
+    legs.got("v1")
+    vbuf[4] = vbuf[2] + vbuf[3]
+    legs.start("v2")
+    a_all(0, 4)
+    a_all(2, 3)
+    legs.got("v2")
+    vbuf[6 + z] = vbuf[4] + vbuf[5]
+    legs.start(*[("v3", i) for i in (1, 2, 3)])
+    for s in range(segs):
+        ig_o[s] = r1f[pl.ds(s * rows, seg_rows), :]
+    a_all(1, 4)
+    legs.got(*[("v3", i) for i in (1, 2, 3)])
+    gv_ref[...] = ((vbuf[6] + vbuf[7]) + vbuf[8]) + vbuf[9]
+    a_all(2, 4)
+    for key in legs.make:
+        if isinstance(key, tuple) and isinstance(key[0], tuple):
+            continue
+        legs.sent(key)
+    for key in units:
+        att_sent(key)
+
+
+def backward(lengths, tokens, w, q, k, v, c, dr1, dup, ddn, lse, dvec):
+    segs, seg_rows, width = tokens.shape
+    rows = q.shape[1]
+    total = segs * rows
+    part = w.shape[-2]
+    half = part // 2
+    pw = 2 * HEAD_DIM
+    sd = jax.ShapeDtypeStruct
+    any_, vm = pl.BlockSpec(memory_space=pl.ANY), whole()
+    V = lambda *s, t=BF: pltpu.VMEM(s, t)
+    nu = width // pw
+    scratch = [V(*w.shape), V(total, width), V(total, width), V(total, width), V(total, width), V(total, width, t=F32), V(segs, seg_rows, width), V(total, width), V(width, total), V(total, width)]
+    scratch += [V(2, 2, 4, 2, half, width)] * 4 + [V(4, 2, half, width), V(2, 4, half, width)] * 2 + [V(4, 4, half, width), V(4, 3, half, width)]
+    scratch += [V(nu, 3, 2, 2, part, pw), V(nu, 3, 2, part, pw), V(nu, 3, part, pw), V(nu, 3, part, pw)]
+    scratch += [V(2, 2, 2, part, width // 2), V(2, 2, part, width // 2), V(2, part, width // 2), V(2, 3, part, width // 2), V(10, 16, width, t=F32)]
+    return pl.pallas_call(
+        functools.partial(backward_kernel, seg_rows),
+        in_specs=[pl.BlockSpec(memory_space=pltpu.SMEM)] + [any_] * 9 + [vm, vm],
+        out_specs=[vm] * 5,
+        out_shape=[sd(tokens.shape, F32)] + [sd((part, width), F32)] * 3 + [sd((16, width), F32)],
+        scratch_shapes=scratch + [DMA((N_BACK_LEGS,)), DMA((N_BACK_LEGS,)), DMA((15,))],
+        compiler_params=pltpu.CompilerParams(collective_id=1, has_side_effects=True, vmem_limit_bytes=63 << 20),
+        name="attention_backward_and_sums",
+    )(lengths, tokens, w, q, k, v, c, dr1, dup, ddn, lse, dvec)
+
 STEPS = 5
 beta_first = 0.9
 beta_second = 0.999
@@ -839,7 +947,6 @@
         block_output, q, k, v, c, w_all, dr1, d_up, d_down, lse, dvec_ffn = forward(
             segment_lengths, tokens, cotangent, attention_master, up_master, down_master, piece
         )
-        w_all = w_all.reshape(4, width, width)
     else:
         low = [m.astype(BF) for m in (attention_master, up_master, down_master)]
         w_all = lax.all_gather(low[0], ("dp", "tensor"), axis=0, tiled=True)
@@ -851,15 +958,14 @@
         down_all = down_all.reshape(tensor_count, width, width)
         q, k, v, c, n1, inv, ab, lse = attn_fwd(segment_lengths, tokens, w_all, table)
         block_output, dr1, d_up, d_down, dvec_ffn = ffn(ab, n1, inv, cotangent, up_all, down_all, table)
-    input_grad, d_attention, dvec_att = attn_bwd(segment_lengths, tokens, w_all, q, k, v, c, lse, dr1)
-    d_vec = dvec_ffn + dvec_att
-
     if own_plan:
-        cut = lambda g, order: g.reshape(tuple(SHAPE[ch] for ch in order) + (4 * width // (dp_count * tensor_count), width))
-        grads = [cut(g, o) for g, o in zip((d_attention, d_up, d_down), ORDERS)]
-        s_attention, s_up, s_down, s_vec = scatter(ORDERS, grads, d_vec)
+        input_grad, s_attention, s_up, s_down, s_vec = backward(
+            segment_lengths, tokens, w_all, q, k, v, c, dr1, d_up, d_down, lse, dvec_ffn
+        )
         s_vec = lax.dynamic_slice_in_dim(s_vec, lax.axis_index("dp") * part, part, axis=1)
     else:
+        input_grad, d_attention, dvec_att = attn_bwd(segment_lengths, tokens, w_all, q, k, v, c, lse, dr1)
+        d_vec = dvec_ffn + dvec_att
         flat = lambda g: g.astype(F32).reshape(-1, width)
         s_attention = lax.psum_scatter(flat(d_attention), ("dp", "tensor"), scatter_dimension=0, tiled=True)
         s_up, s_down = (lax.psum_scatter(flat(g), ("tensor", "dp"), scatter_dimension=0, tiled=True) for g in (d_up, d_down))

time: 286 us -> 253 us (0.88)
  Pallas kernels: 264 us -> 233 us
    pallas_call x2 -> x1, Pallas kernels: 136 us -> 105 us  [backward(): pl.pallas_call(functools.partial(backward_kernel, seg_rows), in_specs=[pl...]
where the time goes in v1:
time: 253 us; the launch traced here: 252 us
  Pallas kernels  233 us (92%)
  local copies, waits for them, and re-layouts  15 us (6%)
  other arithmetic  3.96 us (2%)
    pallas_call x1, Pallas kernels, forward(): pl.pallas_call(functools.partial(forward_kernel, seg_rows), in_specs=[pl....  128 us
    pallas_call x1, Pallas kernels, backward(): pl.pallas_call(functools.partial(backward_kernel, seg_rows), in_specs=[pl...  105 us
    unnamed x36, local copies, waits for them, and re-layouts  14.4 us

profile of v1, /device:TPU:0, one launch (start us, length us, event | category | flops | bytes accessed | tf_op | source)
XLA Modules:
  0.0 252.3 jit_solution(8544335427402221676)
XLA Ops:
  0.6 0.0 copy-start
  0.7 2.9 %copy.29.tok = bf16[2,532,768]{2,1,0:T(8,128)(2,1)} copy(bf16[2,532,768]{2,0,1:T(2,128)(2,1)} %param.15) | data formatting | bytes 3268608 | tf_op args[0]
  3.6 0.0 copy-done
  3.6 0.0 copy-start.13
  3.6 1.4 copy.30.cot
  5.0 0.0 copy-done.13
  5.0 0.6 pad.4.vp
  5.6 127.9 %forward_and_feed_forward_backward.1 = (bf16[2,532,768]{2,1,0:T(8,128)(2,1)}, bf16[2,544,768]{2,1,0:T(8,128)(2,1)}, bf16[2,544,768]{2,1,0:T(8,128)(2,1)}, bf16[2...) custom-call(s32[2]{0:T(128)} %len_ref.3, ...), custom_call_target="tpu_custom_call" | custom-call | tf_op jit(solution)/shard_map/forward_and_feed_forward_backward/pallas_call | solution.py:571
  133.6 3.9 %copy.32 = bf16[2,532,768]{2,0,1:T(2,128)(2,1)} copy(bf16[2,532,768]{2,1,0:T(8,128)(2,1)} %get-tuple-element.46) | data formatting | bytes 3268608
  137.4 104.6 %attention_backward_and_sums.1 = (f32[2,532,768]{2,1,0:T(8,128)}, f32[96,768]{1,0:T(8,128)}, f32[96,768]{1,0:T(8,128)}, f32[96,768]{1,0:T(8,128)}, f32[16,768]{1,0:T(8,128)}) custom-call(s32[2]{0:T(128)} %len_ref.3, bf16[2,532,768]{2,1,0:T(8,128)(2,1)} %copy.29.tok, bf16[4,2,2,2,96,768]{5,4,3,2,1,0:T(8,128)(2,1)} %get-tuple-element.31.w_i, ...), custom_call_target="tpu_custom_call" | custom-call | tf_op jit(solution)/shard_map/attention_backward_and_sums/pallas_call | solution.py:893
  242.0 0.0 copy-start.3
  242.0 0.0 copy-start.10
  242.1 0.0 copy-start.11
  242.1 0.0 copy-start.12
  242.1 0.0 copy-start.9
  242.1 5.4 %copy.33 = f32[2,532,768]{2,0,1:T(2,128)} copy(f32[2,532,768]{2,1,0:T(8,128)} %get-tuple-element.47) | data formatting | bytes 6537216
  247.5 0.0 copy-start.1
  247.5 0.0 copy-start.2
  247.5 0.0 copy-start.4
  247.5 0.0 copy-start.5
  247.5 0.0 copy-start.6
  247.5 0.0 copy-start.7
  247.5 0.0 copy-start.8
  247.6 0.0 copy-done.3
  247.6 0.0 copy-done.10
  247.6 0.0 copy-done.11
  247.6 0.0 copy-done.12
  247.6 1.0 multiply_subtract_fusion.2
  248.6 0.0 copy-done.9
  248.6 0.0 copy-done.1
  248.6 0.0 copy-done.2
  248.6 0.2 copy-done.4
  248.8 0.2 copy-done.5
  249.1 0.1 copy-done.6
  249.1 0.1 copy-done.7
  249.2 0.1 copy-done.8
  249.3 0.0 copy-start.14
  249.3 0.0 copy-start.15
  249.3 1.5 multiply_subtract_fusion
  250.8 0.0 copy-done.14
  250.8 0.0 copy-done.15
  250.8 1.4 multiply_subtract_fusion.3
  (1 shorter events, 0.0 us)
Async XLA Ops:
  0.6 2.9 %copy-start = (bf16[2,532,768]{2,0,1:T(2,128)(2,1)S(1)}, bf16[2,532,768]{2,0,1:T(2,128)(2,1)}, u32[]{:S(2)}) copy-start(bf16[2,532,768]{2,0,1:T(2,128)(2,1)} %param.17) | copy-start | bytes 4902916
  3.6 1.5 copy-start.13
  242.0 5.5 %copy-start.3 = (f32[96,768]{1,0:T(8,128)S(1)}, f32[96,768]{1,0:T(8,128)}, u32[]{:S(2)}) copy-start(f32[96,768]{1,0:T(8,128)} %am.1) | copy-start | bytes 884740
  242.0 5.5 %copy-start.10 = (f32[96,768]{1,0:T(8,128)S(1)}, f32[96,768]{1,0:T(8,128)}, u32[]{:S(2)}) copy-start(f32[96,768]{1,0:T(8,128)} %param.19) | copy-start | bytes 884740
  242.1 5.5 %copy-start.11 = (f32[96,768]{1,0:T(8,128)S(1)}, f32[96,768]{1,0:T(8,128)}, u32[]{:S(2)}) copy-start(f32[96,768]{1,0:T(8,128)} %param.20) | copy-start | bytes 884740
  242.1 5.5 %copy-start.12 = (f32[96,768]{1,0:T(8,128)S(1)}, f32[96,768]{1,0:T(8,128)}, u32[]{:S(2)}) copy-start(f32[96,768]{1,0:T(8,128)} %get-tuple-element.42) | copy-start | bytes 884740
  242.1 6.6 %copy-start.9 = (f32[96,768]{1,0:T(8,128)S(1)}, f32[96,768]{1,0:T(8,128)}, u32[]{:S(2)}) copy-start(f32[96,768]{1,0:T(8,128)} %get-tuple-element.44) | copy-start | bytes 884740
  247.5 1.1 copy-start.1
  247.5 1.1 copy-start.2
  247.5 1.3 copy-start.4
  247.5 1.5 copy-start.5
  247.5 1.6 copy-start.6
  247.5 1.7 copy-start.7
  247.5 1.8 copy-start.8
  249.3 1.5 copy-start.14
  249.3 1.5 copy-start.15

commit v2 on v1

--- a/solution.py
+++ b/solution.py
@@ -241,43 +241,41 @@
     )(lengths, tokens, weights, q, k, v, c, lse, dr1)
 
 MESH = pl.DeviceIdType.MESH
-F32, BF = jnp.float32, jnp.bfloat16
 DMA = pltpu.SemaphoreType.DMA
+SHAPE = {"z": 4, "x": 2, "y": 2, "c": 2}
+ATT, FFN = "zxyc", "yczx"
+ROUTES = ("zxy", "zyx", "xzy", "zyx", "zxy", "yzx")
+
 
 def place():
     d, t = lax.axis_index("dp"), lax.axis_index("tensor")
     return d // 2, d % 2, t // 2, t % 2
 
+
 def dev(z, x, y, c):
     return {"dp": z * 2 + x, "tensor": y * 2 + c}
 
-def greet(z, x, y, c):
+
+def partners(z, x, y, c):
+    return {"x": (z, 1 - x, y, c), "y": (z, x, 1 - y, c), "c": (z, x, y, 1 - c), **{i: ((z + i) % 4, x, y, c) for i in (1, 2, 3)}}
+
+
+def greet(*here):
     b = pltpu.get_barrier_semaphore()
-    for p in [((z + k) % 4, x, y, c) for k in (1, 2, 3)] + [(z, 1 - x, y, c), (z, x, 1 - y, c), (z, x, y, 1 - c)]:
+    for p in partners(*here).values():
         pl.semaphore_signal(b, inc=1, device_id=dev(*p), device_id_type=MESH)
     pl.semaphore_wait(b, 6)
 
-def pick(ref, order, rows=None, **at):
-    idx = tuple(at.get(ch, slice(None)) for ch in order)
-    return ref.at[idx + ((rows,) if rows is not None else ())]
-
-def send(src, dst, s, r, p):
-    cp = pltpu.make_async_remote_copy(src, dst, s, r, device_id=dev(*p), device_id_type=MESH)
-    cp.start()
-    return cp
-
-SHAPE = {"z": 4, "x": 2, "y": 2, "c": 2}
-
 
 class Legs:
-    def __init__(self, ssem, rsem):
-        self.ssem, self.rsem, self.make, self.count = ssem, rsem, {}, 0
+    def __init__(self, here, ssem, rsem):
+        self.here, self.peer = dict(zip("zxyc", here)), partners(*here)
+        self.ssem, self.rsem, self.make = ssem, rsem, {}
 
     def add(self, key, src, dst, peer):
-        i = self.count
-        self.count += 1
+        i = len(self.make)
         self.make[key] = lambda: pltpu.make_async_remote_copy(
-            src(), dst(), self.ssem.at[i], self.rsem.at[i], device_id=dev(*peer), device_id_type=MESH)
+            src(), dst(), self.ssem.at[i], self.rsem.at[i], device_id=dev(*self.peer[peer]), device_id_type=MESH)
 
     def start(self, *keys):
         for k in keys:
@@ -287,27 +285,112 @@
         for k in keys:
             self.make[k]().wait_recv()
 
-    def sent(self, *keys):
-        for k in keys:
-            self.make[k]().wait_send()
-
-def add_spread(legs, key, view, place_now, h):
-    z, x, y, c = place_now
-    core, xp, yp = (z, x, y, 1 - c), (z, 1 - x, y, c), (z, x, 1 - y, c)
-    def leg(name, peer, **at):
-        legs.add((key, name), lambda: view(**at), lambda: view(**at), peer)
-    leg("s1", xp if h == 0 else yp, x=x, y=y, c=c)
-    leg("k1", core, x=x, y=y, c=c)
-    if h == 0:
-        leg("s2", yp, y=y, c=c)
-        leg("k2", core, x=1 - x, y=y, c=c)
-        leg("k3", core, y=1 - y, c=c)
-    else:
-        leg("s2", xp, x=x, c=c)
-        leg("k2", core, x=x, y=1 - y, c=c)
-        leg("k3", core, x=1 - x, c=c)
-
-N_FORWARD_LEGS = 3 * 3 + 4 + 6 * 5 + 2 * 5 + 4 * 3 + 4 * 5
+    def sent(self):
+        for m in self.make.values():
+            m().wait_send()
+
+
+def view_of(ref, order, cols):
+    return lambda at, rows: ref.at[tuple(at.get(ch, slice(None)) for ch in order) + (rows, cols)]
+
+
+class GatherUnit:
+    def __init__(self, legs, key, view, r0, nr, route):
+        self.legs, self.key, self.steps = legs, key, [([], [])]
+        me = legs.here
+        c = {"c": me["c"]}
+        full = pl.ds(r0, nr)
+
+        def leg(name, peer, at):
+            f = functools.partial(view, at, full)
+            legs.add((key, name), f, f, peer)
+            self.steps[-1][1].append((key, name))
+
+        for n, d in enumerate(route + "c"):
+            fixed = {**c, **{e: me[e] for e in route[n:]}}
+            names = [(d, i) for i in (1, 2, 3)] if d == "z" else [(d, d)]
+            for name in names:
+                leg(name, name[1], fixed)
+            self.steps.append(([(key, name) for name in names], []))
+
+    def go(self, n):
+        self.legs.got(*self.steps[n][0])
+        self.legs.start(*self.steps[n][1])
+
+
+class SumUnit:
+    @staticmethod
+    def buffers(order, nr, nc, route):
+        inner = order.replace("c", "")
+        out, gone = [], ""
+        for d in "c" + route:
+            gone += d
+            out += [tuple(SHAPE[ch] for ch in inner if ch not in gone) + (nr, nc)] * (3 if d == "z" else 1)
+        return out
+
+    def __init__(self, legs, key, given, own, bufs, r0, nr, order, route, finish, ready=None):
+        self.legs, self.key, self.own, self.finish, self.ready = legs, key, own, finish, ready
+        self.inner = order.replace("c", "")
+        self.rows = pl.ds(r0, nr)
+        me, bufs, done = legs.here, list(bufs), {"c": legs.here["c"]}
+        self.work = []
+        for d in "c" + route:
+            names = [(d, i) for i in (1, 2, 3)] if d == "z" else [(d, d)]
+            got = []
+            for name in names:
+                to = (me["z"] + name[1]) % 4 if d == "z" else 1 - me[d]
+                b = bufs.pop(0)
+                got.append(b)
+                legs.add((key, name), functools.partial(given if d == "c" else own, {**done, d: to}, self.rows), functools.partial(lambda b: b, b), name[1])
+            done = {**done, d: me[d]}
+            self.work.append(([(key, name) for name in names], dict(done), got))
+
+    def begin(self):
+        self.legs.start(*self.work[0][0])
+
+    def go(self, n):
+        names, at, bufs = self.work[n]
+        self.legs.got(*names)
+        if n == 0 and self.ready is not None:
+            self.ready()
+        free = [ch for ch in self.inner if ch not in at]
+
+        def total(ref, cut):
+            t = ref[...].astype(jnp.float32)
+            for b in bufs:
+                t = t + cut(b).astype(jnp.float32)
+            return t
+        if n == len(self.work) - 1:
+            self.finish(self.rows, total(self.own(at, self.rows), lambda b: b[...]))
+            return
+        ch = free[0]
+
+        def body(i, carry):
+            ref = self.own({**at, ch: i}, self.rows)
+            ref[...] = total(ref, lambda b: b[i]).astype(jnp.bfloat16)
+            return carry
+        lax.fori_loop(0, SHAPE[ch], body, 0)
+        self.legs.start(*self.work[n + 1][0])
+
+
+N_FORWARD_LEGS = 18 * 6 + 4
+GATHER_FIRST = ((0, 0),), ((0, 1), (1, 0)), ((0, 2), (2, 0)), ((0, 3), (1, 1), (3, 0), (4, 0), (5, 0))
+GATHER_SLOTS = {
+    0: ((1, 2), (2, 1)),
+    4: ((1, 3), (2, 2), (3, 1)),
+    6: ((4, 1),),
+    8: ((1, 4), (5, 1), (6, 0)),
+    10: ((2, 3), (3, 2), (7, 0)),
+    12: ((4, 2), (8, 0)),
+    14: ((5, 2), (6, 1)),
+    16: ((2, 4), (3, 3), (7, 1)),
+    18: ((4, 3), (6, 2), (8, 1)),
+    20: ((5, 3), (7, 2)),
+    24: ((6, 3), (8, 2)),
+    28: ((7, 3),),
+    32: ((8, 3),),
+}
+
 
 def forward_kernel(seg_rows, len_ref, tok, cot, am, um, dm, vp,
                    out_o, q_o, k_o, v_o, c_o, w_o, dr1_o, dup_o, ddn_o, lse_ref, dvec_ref,
@@ -318,7 +401,6 @@
     heads = width // HEAD_DIM
     part = am.shape[0]
     z, x, y, c = here = place()
-    peers_z = {i: ((z + i) % 4, x, y, c) for i in (1, 2, 3)}
     lt = pltpu.make_async_copy(tok, traw, lsem.at[0]); lt.start()
     lc = pltpu.make_async_copy(cot, craw, lsem.at[1]); lc.start()
     wa[z, x, y, c] = am[...].astype(BF)
@@ -326,82 +408,39 @@
     wd[y, c, z, x] = dm[...].astype(BF)
     vec[z, x] = vp[...]
 
-    legs = Legs(ssem, rsem)
+    legs = Legs(here, ssem, rsem)
     pair_w = 2 * HEAD_DIM
     groups = width // (2 * pair_w)
-    for g in range(groups):
-        col = pl.ds(g * 2 * pair_w, 2 * pair_w)
-        for i in (1, 2, 3):
-            f = functools.partial(lambda col: wa.at[z, x, y, c, :, col], col)
-            legs.add(("z", g, i), f, f, peers_z[i])
+    units = []
+    for name, ref, order in (("a", wa, ATT), ("u", wu, FFN), ("d", wd, FFN)):
+        for h in range(2 * groups):
+            units.append(GatherUnit(legs, (name, h), view_of(ref, order, pl.ds(h * pair_w, pair_w)), 0, part, ROUTES[h]))
+    here_vec = lambda: vec.at[z, x]
     for i in (1, 2, 3):
-        legs.add(("vz", i), lambda: vec.at[z, x], lambda: vec.at[z, x], peers_z[i])
-    legs.add("vx", lambda: vec.at[:, x], lambda: vec.at[:, x], (z, 1 - x, y, c))
-    three = pl.ds(0, 3)
-    def att_view(zz, col):
-        return lambda **at: pick(wa, "zxycr", z=zz, **at).at[(Ellipsis,)] if False else wa.at[tuple([zz] + [at.get(ch, slice(None)) for ch in "xyc"] + [slice(None), col])]
-    for g in range(groups):
-        for h in range(2):
-            add_spread(legs, ("a", g, h), att_view(three, pl.ds((2 * g + h) * pair_w, pair_w)), here, h)
-    for h in range(2):
-        add_spread(legs, ("o", h), att_view(3, pl.ds(h * (width // 2), width // 2)), here, h)
-    half = part // 2
-    for name, ref in (("u", wu), ("d", wd)):
-        for h in range(2):
-            rr = pl.ds(h * half, half)
-            f = functools.partial(lambda ref, rr: ref.at[y, c, z, x, rr], ref, rr)
-            for i in (1, 2, 3):
-                legs.add((name, h, "z", i), f, f, peers_z[i])
-            view = functools.partial(lambda ref, rr, **at: ref.at[tuple([at.get(ch, slice(None)) for ch in "yczx"] + [rr])], ref, rr)
-            add_spread(legs, (name, h), view, here, h)
-
-    def stage(units, n):
-        for u in units:
-            if n == 2:
-                legs.got((u, "s1"))
-                legs.start((u, "s2"), (u, "k2"))
-            elif n == 3:
-                legs.got((u, "s2"))
-                legs.start((u, "k3"))
-            elif n == 1:
-                legs.start((u, "s1"), (u, "k1"))
-            elif n == 4:
-                legs.got((u, "k1"), (u, "k2"), (u, "k3"))
-    A = lambda g: [("a", g, 0), ("a", g, 1)]
-    O = [("o", 0), ("o", 1)]
-    U, W = [("u", 0), ("u", 1)], [("d", 0), ("d", 1)]
-    def zstart(name):
-        for h in range(2):
-            legs.start(*[(name, h, "z", i) for i in (1, 2, 3)])
-    def zgot(name):
-        for h in range(2):
-            legs.got(*[(name, h, "z", i) for i in (1, 2, 3)])
+        legs.add(("v", i), here_vec, here_vec, i)
+    legs.add("vx", lambda: vec.at[:, x], lambda: vec.at[:, x], "x")
+
+    def advance(what):
+        for i, n in what:
+            for unit in units[2 * i:2 * i + 2]:
+                unit.go(n)
 
     greet(*here)
-    legs.start(*[("z", 0, i) for i in (1, 2, 3)])
-    legs.start(*[("vz", i) for i in (1, 2, 3)])
-    for g in range(1, groups):
-        legs.start(*[("z", g, i) for i in (1, 2, 3)])
+    advance(GATHER_FIRST[0])
+    legs.start(*[("v", i) for i in (1, 2, 3)])
     lt.wait()
     for s in range(segs):
         xs[pl.ds(s * rows, seg_rows), :] = traw[s]
         xs[pl.ds(s * rows + seg_rows, rows - seg_rows), :] = jnp.zeros((rows - seg_rows, width), BF)
-    legs.got(*[("z", 0, i) for i in (1, 2, 3)])
-    stage(A(0), 1)
+    advance(GATHER_FIRST[1])
+    legs.got(*[("v", i) for i in (1, 2, 3)])
+    legs.start("vx")
+    advance(GATHER_FIRST[2])
     lc.wait()
     for s in range(segs):
         cs[pl.ds(s * rows, seg_rows), :] = craw[s]
         cs[pl.ds(s * rows + seg_rows, rows - seg_rows), :] = jnp.zeros((rows - seg_rows, width), BF)
-    legs.got(*[("z", 1, i) for i in (1, 2, 3)])
-    stage(A(1), 1)
-    stage(A(0), 2)
-    legs.got(*[("vz", i) for i in (1, 2, 3)])
-    legs.start("vx")
-    legs.got(*[("z", 2, i) for i in (1, 2, 3)])
-    stage(A(2), 1)
-    zstart("u")
-    stage(A(1), 2)
-    stage(A(0), 3)
+    advance(GATHER_FIRST[3])
     legs.got("vx")
     lane_in = lax.broadcasted_iota(jnp.int32, (128, width), 0)
     lane_out = lax.broadcasted_iota(jnp.int32, (128, width), 1)
@@ -410,24 +449,15 @@
         move = ((lane_out == lane_in + d * part) & (lane_in < part)).astype(BF)
         acc = acc + mm(vec[d // 2, d % 2], move)
     tab[...] = acc
-    ticks = {
-        1: lambda: (stage(A(2), 2), stage(A(1), 3)),
-        2: lambda: (stage(O, 1), stage(A(2), 3)),
-        3: lambda: (stage(O, 2), zgot("u"), stage(U, 1)),
-        5: lambda: (stage(O, 3), stage(U, 2), zstart("d")),
-        8: lambda: (zgot("d"), stage(W, 1)),
-        9: lambda: stage(U, 3),
-        11: lambda: stage(W, 2),
-    }
+    advance(((0, 4),))
     lane = lax.broadcasted_iota(jnp.int32, (rows, pair_w), 1)
     key_at = lax.broadcasted_iota(jnp.int32, (rows, 1), 0)
     zero = jnp.zeros((), BF)
 
     def body(it, carry):
-        for n, f in ticks.items():
-            pl.when(it == n)(lambda f=f: (f(), None)[1])
-        for g in range(groups):
-            pl.when(it == 4 * g)(lambda g=g: (stage(A(g), 4), None)[1])
+        for n in range(0, 8 * groups, 2):
+            if n in GATHER_SLOTS:
+                pl.when(2 * it == n)(functools.partial(lambda n: advance(GATHER_SLOTS[n]), n))
         g = it // 4
 
         @pl.when(it % 4 == 0)
@@ -450,6 +480,10 @@
         vt = v2.T
         for h in range(2):
             mine = (lane < HEAD_DIM) if h == 0 else (lane >= HEAD_DIM)
+            if h == 1:
+                for n in range(1, 8 * groups, 2):
+                    if n in GATHER_SLOTS:
+                        pl.when(2 * it + 1 == n)(functools.partial(lambda n: advance(GATHER_SLOTS[n]), n))
             sc = mm(k2, jnp.where(mine, q2, zero), NT) + bias
             top = jnp.max(sc, axis=0, keepdims=True)
             e = jnp.exp(sc - top)
@@ -464,7 +498,6 @@
     spill = [pltpu.make_async_copy(a.at[pl.ds(s * rows, rows)], o.at[s], lsem.at[2 + 2 * n + s]) for n, (a, o) in enumerate(((q, q_o), (k, k_o), (v, v_o))) for s in range(segs)]
     for cp in spill:
         cp.start()
-    stage(O, 4)
     wcopy = pltpu.make_async_copy(wa, w_o, lsem.at[8]); wcopy.start()
     for s in range(segs):
         rr = pl.ds(s * rows, rows)
@@ -488,18 +521,21 @@
         return wu[j // 2, j % 2].reshape(width, width)
     def down(j):
         return wd[j // 2, j % 2].reshape(width, width)
-    stage(U, 4)
+    advance(((3, 4), (4, 4), (5, 4)))
+
     def fwd(i, carry):
-        pl.when(i == 2)(lambda: (stage(W, 3), None)[1])
         a = ab[rb(i), :]
         for j in range(chunks):
+            for n in range(nb):
+                if 8 * groups + 4 * n + j in GATHER_SLOTS:
+                    pl.when(i == n)(functools.partial(lambda n: advance(GATHER_SLOTS[n]), 8 * groups + 4 * n + j))
             u = mm(a, up(j)) + tab[8 + j:9 + j, :]
             phi = 0.5 * (1.0 + lax.erf(u * inv_root_two))
             hid[j, rb(i), :] = (u * phi).astype(BF)
             slo[j, rb(i), :] = (phi + u * jnp.exp(-0.5 * u * u) * inv_root_tau).astype(BF)
         return carry
     lax.fori_loop(0, nb, fwd, 0)
-    stage(W, 4)
+    advance(((6, 4), (7, 4), (8, 4)))
     dvec_ref[...] = jnp.zeros_like(dvec_ref)
     def mid(i, carry):
         yy = tab[7:8, :]
@@ -536,7 +572,7 @@
     ocopy = pltpu.make_async_copy(craw, out_o, lsem.at[1]); ocopy.start()
     dyt[...] = dy[...].T
     abt[...] = ab[...].T
-    legs.sent(*legs.make)
+    legs.sent()
     def grad_copies(j):
         return (pltpu.make_async_copy(wd.at[j // 2, j % 2], ddn_o.at[j // 2, j % 2], lsem.at[11 + 2 * (j % 2)]),
                 pltpu.make_async_copy(wu.at[j // 2, j % 2], dup_o.at[j // 2, j % 2], lsem.at[12 + 2 * (j % 2)]))
@@ -581,28 +617,27 @@
         name="forward_and_feed_forward_backward",
     )(lengths, tokens, cotangent, att, up, down, piece)
 
-N_BACK_LEGS = 4 * 6 + 2 * 6 + 6 * 6 + 6
-
-
-def backward_kernel(seg_rows, len_ref, tok, w_i, q_i, k_i, v_i, c_i, dr1_i, dup, ddn, lse_ref, dvec_in,
+N_BACK_LEGS = 18 * 6 + 6
+SUM_SLOTS = ((0, 4, 8, 12),) * 3 + ((4, 10, 16, 22),) * 3 + ((10, 16, 22, 24), (18, 22, 25, 27), (24, 26, 28, 30))
+
+
+def sum_plan(width):
+    pw = 2 * HEAD_DIM
+    return [((name, h), h * pw, pw, order, ROUTES[h][::-1]) for name, order in (("u", FFN), ("d", FFN), ("a", ATT)) for h in range(width // pw)]
+
+
+def backward_kernel(seg_rows, n_bufs, len_ref, tok, w_i, q_i, k_i, v_i, c_i, dr1_i, dup, ddn, lse_ref, dvec_in,
                     ig_o, ga_ref, gu_ref, gd_ref, gv_ref,
-                    wa, q, k, v, cc, r1f, traw, xs, xt, dao, own_u, own_d, rc_u, rc_d, h1_u0, h1_u1, h1_d0, h1_d1, h2_f, rz_f, rc_a, h1_a, h2_a, rz_a, rc_o, h1_o, h2_o, rz_o, vbuf,
-                    ssem, rsem, lsem):
+                    wa, ga, q, k, v, cc, r1f, traw, xt, dao, own_u, own_d, vbuf, *rest):
+    bufs, (ssem, rsem, lsem) = list(rest[:n_bufs]), rest[n_bufs:]
     segs, rows, width = q_i.shape
     total = segs * rows
     heads = width // HEAD_DIM
     pair_w = 2 * HEAD_DIM
     groups = width // (2 * pair_w)
     part = ga_ref.shape[0]
-    half = part // 2
     z, x, y, c = here = place()
-    me = dict(z=z, x=x, y=y, c=c)
-    core, xp, yp = (z, x, y, 1 - c), (z, 1 - x, y, c), (z, x, 1 - y, c)
-    zp = {i: ((z + i) % 4, x, y, c) for i in (1, 2, 3)}
-    h1_u, h1_d = (h1_u0, h1_u1), (h1_d0, h1_d1)
-    legs = Legs(ssem, rsem)
-    first, second = {0: "y", 1: "x"}, {0: "x", 1: "y"}
-    peer = {"x": xp, "y": yp}
+    legs = Legs(here, ssem, rsem)
 
     load = {}
     def local(name, src, dst, i):
@@ -618,187 +653,82 @@
         local(("q", s), q_i.at[s], q.at[rr], 8 + s)
     local("t", tok, traw, 10)
 
-    ff = [("u", dup, own_u, rc_u, h1_u), ("d", ddn, own_d, rc_d, h1_d)]
-    hop = {}
-    for n, (name, g, own, rc, h1) in enumerate(ff):
-        for h in range(2):
-            rr = pl.ds(h * half, half)
-            u = 2 * n + h
-            f, s = first[h], second[h]
-            o = own.at[h]
-            legs.add((name, h, 0), functools.partial(lambda g, rr: g.at[:, 1 - c, :, :, rr], g, rr), functools.partial(lambda rc, h: rc.at[h], rc, h), core)
-            local((name, h), g.at[:, c, :, :, rr], o, 11 + u)
-            legs.add((name, h, 1), functools.partial(lambda o, f: pick(o, "yzx", **{f: 1 - me[f]}), o, f), functools.partial(lambda h1, h: h1[h], h1, h), peer[f])
-            legs.add((name, h, 2), functools.partial(lambda o, f, s: pick(o, "yzx", **{f: me[f], s: 1 - me[s]}), o, f, s), functools.partial(lambda u: h2_f.at[u], u), peer[s])
-            for i in (1, 2, 3):
-                legs.add((name, h, 2 + i), functools.partial(lambda o, i: o.at[y, (z + i) % 4, x], o, i), functools.partial(lambda u, i: rz_f.at[u, i - 1], u, i), zp[i])
-
-    def ff_stage(name, h, n):
-        own, rc, h1 = (own_u, rc_u, h1_u) if name == "u" else (own_d, rc_d, h1_d)
-        u = 2 * (name == "d") + h
-        o, f, s = own.at[h], first[h], second[h]
-        if n == 0:
-            legs.got((name, h, 0))
-            load[name, h].wait()
-            def body(i, _):
-                at = (i // 8, (i // 2) % 4, i % 2)
-                o[at] = (o[at].astype(F32) + rc[(h,) + at].astype(F32)).astype(BF)
-                return 0
-            lax.fori_loop(0, 16, body, 0)
-            legs.start((name, h, 1))
-        elif n == 1:
-            legs.got((name, h, 1))
-            left = "yzx".replace(f, "")
-            sh = [SHAPE[ch] for ch in left]
-            o = pick(o, "yzx", **{f: me[f]})
-            def body(i, _):
-                at = (i // sh[1], i % sh[1])
-                o[at] = (o[at].astype(F32) + h1[h][at].astype(F32)).astype(BF)
-                return 0
-            lax.fori_loop(0, 8, body, 0)
-            legs.start((name, h, 2))
-        elif n == 2:
-            legs.got((name, h, 2))
-            def body(i, _):
-                o[y, i, x] = (o[y, i, x].astype(F32) + h2_f[u, i].astype(F32)).astype(BF)
-                return 0
-            lax.fori_loop(0, 4, body, 0)
-            legs.start(*[(name, h, 2 + i) for i in (1, 2, 3)])
+    local("u", dup.at[:, c], own_u, 11)
+    local("d", ddn.at[:, c], own_d, 12)
+    loaded = set()
+    def need(name):
+        if name not in loaded:
+            loaded.add(name)
+            load[name].wait()
+
+    units = {}
+    for key, c0, nc, order, route in sum_plan(width):
+        mine = bufs[:6]
+        del bufs[:6]
+        col = pl.ds(c0, nc)
+        if key[0] == "a":
+            given = own = view_of(ga, ATT, col)
+            out, ready = ga_ref, None
         else:
-            legs.got(*[(name, h, 2 + i) for i in (1, 2, 3)])
-            out = gu_ref if name == "u" else gd_ref
-            out[pl.ds(h * half, half)] = ((o[y, z, x].astype(F32) + rz_f[u, 0].astype(F32)) + rz_f[u, 1].astype(F32)) + rz_f[u, 2].astype(F32)
-
-    three = pl.ds(0, 3)
-    def att(zz, col, **at):
-        return wa.at[tuple([zz] + [at.get(ch, slice(None)) for ch in "xyc"] + [slice(None), col])]
-    def add_att(key, zz, col, rc, h1, h2, rz, h):
-        f, s = first[h], second[h]
-        legs.add((key, 0), lambda: att(zz, col, c=1 - c), lambda: rc, core)
-        legs.add((key, 1), lambda: att(zz, col, c=c, **{f: 1 - me[f]}), lambda: h1, peer[f])
-        legs.add((key, 2), lambda: att(zz, col, c=c, **{f: me[f], s: 1 - me[s]}), lambda: h2, peer[s])
-        for i in (1, 2, 3):
-            legs.add((key, 2 + i), functools.partial(lambda i: att((z + i) % 4, col, c=c, x=x, y=y), i), functools.partial(lambda i: rz.at[i - 1], i), zp[i])
-    units = {}
-    for g in range(groups):
-        for h in range(2):
-            u = 2 * g + h
-            col = pl.ds(u * pair_w, pair_w)
-            units["a", g, h] = (range(3), col, rc_a.at[u], h1_a.at[u], h2_a.at[u], rz_a.at[u], h)
-            add_att(("a", g, h), three, col, *units["a", g, h][2:])
-    for h in range(2):
-        col = pl.ds(h * (width // 2), width // 2)
-        units["o", h] = ((3,), col, rc_o.at[h], h1_o.at[h], h2_o.at[h], rz_o.at[h], h)
-        add_att(("o", h), 3, col, *units["o", h][2:])
-
-    def att_stage(key, n):
-        zs, col, rc, h1, h2, rz, h = units[key]
-        f, s = first[h], second[h]
-        one = len(zs) == 1
-        base = zs[0]
-        def sub(ref, i, *rest):
-            at = tuple(rest) if one else (i,) + tuple(rest)
-            return ref[at] if at else ref[...]
-        if n == 0:
-            legs.start((key, 0))
-            return
-        if n == 1:
-            legs.got((key, 0))
-            def body(i, _):
-                m, a, b = base + i // 4, (i // 2) % 2, i % 2
-                t = (m, a, b, c, slice(None), col)
-                wa[t] = (wa[t].astype(F32) + sub(rc, i // 4, a, b).astype(F32)).astype(BF)
-                return 0
-            lax.fori_loop(0, 4 * len(zs), body, 0)
-            legs.start((key, 1))
-        elif n == 2:
-            legs.got((key, 1))
-            def body(i, _):
-                m, a = base + i // 2, i % 2
-                t = (m, a, y, c, slice(None), col) if f == "y" else (m, x, a, c, slice(None), col)
-                wa[t] = (wa[t].astype(F32) + sub(h1, i // 2, a).astype(F32)).astype(BF)
-                return 0
-            lax.fori_loop(0, 2 * len(zs), body, 0)
-            legs.start((key, 2))
-        elif n == 3:
-            legs.got((key, 2))
-            def body(i, _):
-                t = (base + i, x, y, c, slice(None), col)
-                wa[t] = (wa[t].astype(F32) + sub(h2, i).astype(F32)).astype(BF)
-                return 0
-            lax.fori_loop(0, len(zs), body, 0)
-            for i in (1, 2, 3):
-                to = (z + i) % 4
-                pl.when((to == 3) if one else (to < 3))(functools.partial(lambda i: (legs.start((key, 2 + i)), None)[1], i))
-        else:
-            @pl.when((z == 3) if one else (z < 3))
-            def _():
-                legs.got(*[(key, 2 + i) for i in (1, 2, 3)])
-                ga_ref[:, col] = ((wa[z, x, y, c, :, col].astype(F32) + rz[0].astype(F32)) + rz[1].astype(F32)) + rz[2].astype(F32)
-
-    def att_sent(key):
-        one = key[0] == "o"
-        legs.sent((key, 0), (key, 1), (key, 2))
-        for i in (1, 2, 3):
-            to = (z + i) % 4
-            pl.when((to == 3) if one else (to < 3))(functools.partial(lambda i: (legs.sent((key, 2 + i)), None)[1], i))
-
-    legs.add("v0", lambda: vbuf.at[0], lambda: vbuf.at[1], core)
-    legs.add("v1", lambda: vbuf.at[2], lambda: vbuf.at[3], yp)
-    legs.add("v2", lambda: vbuf.at[4], lambda: vbuf.at[5], xp)
+            given = view_of(dup if key[0] == "u" else ddn, FFN, col)
+            own = view_of(own_u if key[0] == "u" else own_d, "yzx", col)
+            out, ready = (gu_ref, gd_ref)[key[0] == "d"], functools.partial(need, key[0])
+        def finish(rr, total, out=out, col=col):
+            out[rr, col] = total
+        units[key] = SumUnit(legs, key, given, own, mine, 0, part, order, route, finish, ready)
+    F = lambda i: [("ud"[i // groups], 2 * (i % groups) + h) for h in range(2)]
+    A = lambda g: [("a", 2 * g), ("a", 2 * g + 1)]
+    def begin(keys):
+        for key in keys:
+            units[key].begin()
+    def stage(keys, n):
+        for key in keys:
+            units[key].go(n)
+
+    legs.add("v0", lambda: vbuf.at[0], lambda: vbuf.at[1], "c")
+    legs.add("v1", lambda: vbuf.at[2], lambda: vbuf.at[3], "y")
+    legs.add("v2", lambda: vbuf.at[4], lambda: vbuf.at[5], "x")
     for i in (1, 2, 3):
-        legs.add(("v3", i), lambda: vbuf.at[6 + z], lambda: vbuf.at[6 + z], zp[i])
+        legs.add(("v", i), lambda: vbuf.at[6 + z], lambda: vbuf.at[6 + z], i)
 
     greet(*here)
-    for h in range(2):
-        for name in ("u", "d"):
-            legs.start((name, h, 0))
+    for i in range(2 * groups):
+        begin(F(i))
     load["dr1"].wait()
     dao[...] = r1f[...].astype(BF)
     for s in range(segs):
         load["c", s].wait()
     load["w"].wait()
-    dwo = mm(cc[...].T, dao[...]).astype(BF)
-    dc = mm(dao[...], wa[3].reshape(width, width), NT).astype(BF)
-    cc[...] = dc
-    wa[3] = dwo.reshape(wa.shape[1:])
-    for h in range(2):
-        att_stage(("o", h), 0)
-    ff_stage("u", 0, 0)
-    ff_stage("u", 1, 0)
+    ga[3] = mm(cc[...].T, dao[...]).astype(BF).reshape(ga.shape[1:])
+    cc[...] = mm(dao[...], wa[3].reshape(width, width), NT).astype(BF)
     load["t"].wait()
     for s in range(segs):
-        xs[pl.ds(s * rows, seg_rows), :] = traw[s]
-        xs[pl.ds(s * rows + seg_rows, rows - seg_rows), :] = jnp.zeros((rows - seg_rows, width), BF)
-    xt[...] = xs[...].T
+        dao[pl.ds(s * rows, seg_rows), :] = traw[s]
+        dao[pl.ds(s * rows + seg_rows, rows - seg_rows), :] = jnp.zeros((rows - seg_rows, width), BF)
+    xt[...] = dao[...].T
     for s in range(segs):
         for n in "qkv":
             load[n, s].wait()
+    need("u")
+    need("d")
     vbuf[0] = dvec_in[...]
-
-    def ffs(*what):
-        return lambda: [ff_stage(*w) for w in what]
-    def atts(*what):
-        return lambda: [att_stage(*w) for w in what]
-    ticks = {
-        1: ffs(("u", 0, 1), ("u", 1, 1), ("d", 0, 0), ("d", 1, 0)),
-        3: ffs(("u", 0, 2), ("u", 1, 2)),
-        4: ffs(("d", 0, 1), ("d", 1, 1)),
-        5: ffs(("u", 0, 3), ("u", 1, 3)),
-        6: atts((("o", 0), 1), (("o", 1), 1)),
-        7: ffs(("d", 0, 2), ("d", 1, 2)),
-        8: atts((("o", 0), 2), (("o", 1), 2), (("a", 0, 0), 1), (("a", 0, 1), 1)),
-        9: ffs(("d", 0, 3), ("d", 1, 3)),
-        10: atts((("o", 0), 3), (("o", 1), 3), (("a", 0, 0), 2), (("a", 0, 1), 2)),
-        11: atts((("a", 0, 0), 3), (("a", 0, 1), 3), (("a", 1, 0), 1), (("a", 1, 1), 1)),
-    }
+    ticks = {}
+    for i, slots in enumerate(SUM_SLOTS):
+        for n, at in enumerate(slots):
+            ticks.setdefault(at, []).append((F(i) if i < 2 * groups else A(i - 2 * groups), n))
+    def tail(n):
+        for w in ticks.get(n, ()):
+            stage(*w)
     lane = lax.broadcasted_iota(jnp.int32, (rows, pair_w), 1)
     key_at = lax.broadcasted_iota(jnp.int32, (rows, 1), 0)
     zero = jnp.zeros((), BF)
 
     def body(it, carry):
-        for n, f in ticks.items():
-            pl.when(it == n)(lambda f=f: (f(), None)[1])
+        def tick(h):
+            for n, what in ticks.items():
+                if n % 2 == h and n < 8 * groups:
+                    pl.when(it == n // 2)(functools.partial(lambda what: ([stage(*w) for w in what], None)[1], what))
+        tick(0)
         g = it // 4
         s = (it // 2) % 2
         i = 2 * g + it % 2
@@ -813,6 +743,8 @@
         dkp = jnp.zeros((rows, pair_w), F32)
         dqt = []
         for h in range(2):
+            if h == 1:
+                tick(1)
             mine = (lane < HEAD_DIM) if h == 0 else (lane >= HEAD_DIM)
             qh = jnp.where(mine, q2, zero)
             gh = jnp.where(mine, g2, zero)
@@ -830,49 +762,42 @@
         def _():
             gcol = pl.ds(pl.multiple_of(g * 2 * pair_w, 2 * pair_w), 2 * pair_w)
             for m, ref in enumerate((q, k, v)):
-                d = ref[:, gcol]
-                r1f[...] += mm(d, wa[m, :, :, :, :, gcol].reshape(width, 2 * pair_w), NT)
-                wa[m, :, :, :, :, gcol] = mm(xt[...], d).astype(BF).reshape(2, 2, 2, part, 2 * pair_w)
+                ga[m, :, :, :, :, gcol] = mm(xt[...], ref[:, gcol]).astype(BF).reshape(2, 2, 2, part, 2 * pair_w)
             for gg in range(groups):
-                pl.when(g == gg)(functools.partial(lambda gg: ([att_stage(("a", gg, h), 0) for h in range(2)], None)[1], gg))
+                pl.when(g == gg)(functools.partial(lambda gg: (begin(A(gg)), None)[1], gg))
         return carry
     lax.fori_loop(0, 4 * groups, body, 0)
 
+    def rest_of_rows(s):
+        at = pl.ds(s * rows, rows)
+        r = r1f[at, :]
+        for m, ref in enumerate((q, k, v)):
+            r = r + mm(ref[at, :], wa[m].reshape(width, width), NT)
+        ig_o[s] = r[:seg_rows]
     vbuf[0, 0:1, :] = jnp.sum(q[...].astype(F32), axis=0, keepdims=True)
     vbuf[0, 1:2, :] = jnp.sum(v[...].astype(F32), axis=0, keepdims=True)
     legs.start("v0")
-    def a_all(g, n):
-        for h in range(2):
-            att_stage(("a", g, h), n)
-    a_all(1, 2)
-    a_all(2, 1)
+    tail(24)
+    tail(25)
     legs.got("v0")
     vbuf[2] = vbuf[0] + vbuf[1]
     legs.start("v1")
-    for h in range(2):
-        att_stage(("o", h), 4)
-    a_all(1, 3)
-    a_all(2, 2)
+    rest_of_rows(0)
+    tail(26)
+    tail(27)
     legs.got("v1")
     vbuf[4] = vbuf[2] + vbuf[3]
     legs.start("v2")
-    a_all(0, 4)
-    a_all(2, 3)
+    rest_of_rows(1)
+    tail(28)
+    tail(29)
     legs.got("v2")
     vbuf[6 + z] = vbuf[4] + vbuf[5]
-    legs.start(*[("v3", i) for i in (1, 2, 3)])
-    for s in range(segs):
-        ig_o[s] = r1f[pl.ds(s * rows, seg_rows), :]
-    a_all(1, 4)
-    legs.got(*[("v3", i) for i in (1, 2, 3)])
+    legs.start(*[("v", i) for i in (1, 2, 3)])
+    tail(30)
+    legs.got(*[("v", i) for i in (1, 2, 3)])
     gv_ref[...] = ((vbuf[6] + vbuf[7]) + vbuf[8]) + vbuf[9]
-    a_all(2, 4)
-    for key in legs.make:
-        if isinstance(key, tuple) and isinstance(key[0], tuple):
-            continue
-        legs.sent(key)
-    for key in units:
-        att_sent(key)
+    legs.sent()
 
 
 def backward(lengths, tokens, w, q, k, v, c, dr1, dup, ddn, lse, dvec):
@@ -880,22 +805,18 @@
     rows = q.shape[1]
     total = segs * rows
     part = w.shape[-2]
-    half = part // 2
-    pw = 2 * HEAD_DIM
     sd = jax.ShapeDtypeStruct
     any_, vm = pl.BlockSpec(memory_space=pl.ANY), whole()
     V = lambda *s, t=BF: pltpu.VMEM(s, t)
-    nu = width // pw
-    scratch = [V(*w.shape), V(total, width), V(total, width), V(total, width), V(total, width), V(total, width, t=F32), V(segs, seg_rows, width), V(total, width), V(width, total), V(total, width)]
-    scratch += [V(2, 2, 4, 2, half, width)] * 4 + [V(4, 2, half, width), V(2, 4, half, width)] * 2 + [V(4, 4, half, width), V(4, 3, half, width)]
-    scratch += [V(nu, 3, 2, 2, part, pw), V(nu, 3, 2, part, pw), V(nu, 3, part, pw), V(nu, 3, part, pw)]
-    scratch += [V(2, 2, 2, part, width // 2), V(2, 2, part, width // 2), V(2, part, width // 2), V(2, 3, part, width // 2), V(10, 16, width, t=F32)]
+    scratch = [V(*w.shape), V(*w.shape)] + [V(total, width)] * 4 + [V(total, width, t=F32), V(segs, seg_rows, width), V(width, total), V(total, width)]
+    scratch += [V(2, 4, 2, part, width)] * 2 + [V(10, 16, width, t=F32)]
+    bufs = [V(*s) for _, _, nc, order, route in sum_plan(width) for s in SumUnit.buffers(order, part, nc, route)]
     return pl.pallas_call(
-        functools.partial(backward_kernel, seg_rows),
+        functools.partial(backward_kernel, seg_rows, len(bufs)),
         in_specs=[pl.BlockSpec(memory_space=pltpu.SMEM)] + [any_] * 9 + [vm, vm],
         out_specs=[vm] * 5,
         out_shape=[sd(tokens.shape, F32)] + [sd((part, width), F32)] * 3 + [sd((16, width), F32)],
-        scratch_shapes=scratch + [DMA((N_BACK_LEGS,)), DMA((N_BACK_LEGS,)), DMA((15,))],
+        scratch_shapes=scratch + bufs + [DMA((N_BACK_LEGS,)), DMA((N_BACK_LEGS,)), DMA((15,))],
         compiler_params=pltpu.CompilerParams(collective_id=1, has_side_effects=True, vmem_limit_bytes=63 << 20),
         name="attention_backward_and_sums",
     )(lengths, tokens, w, q, k, v, c, dr1, dup, ddn, lse, dvec)

time: 253 us -> 232 us (0.917)
  Pallas kernels: 233 us -> 212 us
    pallas_call x1, Pallas kernels: 105 us -> 91 us  [backward(): pl.pallas_call(functools.partial(backward_kernel, seg_rows, len(bufs)), i...]
    pallas_call x1, Pallas kernels: 128 us -> 121 us  [forward(): pl.pallas_call(functools.partial(forward_kernel, seg_rows), in_specs=[pl....]
where the time goes in v2:
time: 232 us
  Pallas kernels  212 us (91%)
  local copies, waits for them, and re-layouts  15 us (6%)
  other arithmetic  3.96 us (2%)
    pallas_call x1, Pallas kernels, forward(): pl.pallas_call(functools.partial(forward_kernel, seg_rows), in_specs=[pl....  121 us
    pallas_call x1, Pallas kernels, backward(): pl.pallas_call(functools.partial(backward_kernel, seg_rows, len(bufs)), i...  91 us
    unnamed x36, local copies, waits for them, and re-layouts  14.4 us

profile of v2, /device:TPU:0, one launch (start us, length us, event | category | flops | bytes accessed | tf_op | source)
XLA Modules:
  0.0 231.7 jit_solution(14026112791580099574)
XLA Ops:
  0.6 0.0 copy-start
  0.7 2.9 %copy.29.tok = bf16[2,532,768]{2,1,0:T(8,128)(2,1)} copy(bf16[2,532,768]{2,0,1:T(2,128)(2,1)} %param.15) | data formatting | bytes 3268608 | tf_op args[0]
  3.6 0.0 copy-done
  3.6 0.0 copy-start.13
  3.6 1.4 copy.30.cot
  5.0 0.0 copy-done.13
  5.0 0.6 pad.4.vp
  5.6 121.0 %forward_and_feed_forward_backward.1 = (bf16[2,532,768]{2,1,0:T(8,128)(2,1)}, bf16[2,544,768]{2,1,0:T(8,128)(2,1)}, bf16[2,544,768]{2,1,0:T(8,128)(2,1)}, bf16[2...) custom-call(s32[2]{0:T(128)} %len_ref.3, ...), custom_call_target="tpu_custom_call" | custom-call | tf_op jit(solution)/shard_map/forward_and_feed_forward_backward/pallas_call | solution.py:607
  126.6 3.9 %copy.32 = bf16[2,532,768]{2,0,1:T(2,128)(2,1)} copy(bf16[2,532,768]{2,1,0:T(8,128)(2,1)} %get-tuple-element.46) | data formatting | bytes 3268608
  130.5 91.0 %attention_backward_and_sums.1 = (f32[2,532,768]{2,1,0:T(8,128)}, f32[96,768]{1,0:T(8,128)}, f32[96,768]{1,0:T(8,128)}, f32[96,768]{1,0:T(8,128)}, f32[16,768]{1,0:T(8,128)}) custom-call(s32[2]{0:T(128)} %len_ref.3, bf16[2,532,768]{2,1,0:T(8,128)(2,1)} %copy.29.tok, bf16[4,2,2,2,96,768]{5,4,3,2,1,0:T(8,128)(2,1)} %get-tuple-element.31.w_i, ...), custom_call_target="tpu_custom_call" | custom-call | tf_op jit(solution)/shard_map/attention_backward_and_sums/pallas_call | solution.py:814
  221.5 0.0 copy-start.3
  221.5 0.0 copy-start.10
  221.5 0.0 copy-start.11
  221.6 0.0 copy-start.12
  221.6 0.0 copy-start.9
  221.6 5.4 %copy.33 = f32[2,532,768]{2,0,1:T(2,128)} copy(f32[2,532,768]{2,1,0:T(8,128)} %get-tuple-element.47) | data formatting | bytes 6537216
  227.0 0.0 copy-start.1
  227.0 0.0 copy-start.2
  227.0 0.0 copy-start.4
  227.0 0.0 copy-start.5
  227.0 0.0 copy-start.6
  227.0 0.0 copy-start.7
  227.0 0.0 copy-start.8
  227.0 0.0 copy-done.3
  227.1 0.0 copy-done.10
  227.1 0.0 copy-done.11
  227.1 0.0 copy-done.12
  227.1 1.0 multiply_subtract_fusion.2
  228.1 0.0 copy-done.9
  228.1 0.0 copy-done.1
  228.1 0.0 copy-done.2
  228.1 0.2 copy-done.4
  228.3 0.2 copy-done.5
  228.5 0.1 copy-done.6
  228.6 0.1 copy-done.7
  228.7 0.1 copy-done.8
  228.8 0.0 copy-start.14
  228.8 0.0 copy-start.15
  228.8 1.5 multiply_subtract_fusion
  230.3 0.0 copy-done.14
  230.3 0.0 copy-done.15
  230.3 1.4 multiply_subtract_fusion.3
  (1 shorter events, 0.0 us)
Async XLA Ops:
  0.6 2.9 %copy-start = (bf16[2,532,768]{2,0,1:T(2,128)(2,1)S(1)}, bf16[2,532,768]{2,0,1:T(2,128)(2,1)}, u32[]{:S(2)}) copy-start(bf16[2,532,768]{2,0,1:T(2,128)(2,1)} %param.17) | copy-start | bytes 4902916
  3.6 1.5 copy-start.13
  221.5 5.5 %copy-start.3 = (f32[96,768]{1,0:T(8,128)S(1)}, f32[96,768]{1,0:T(8,128)}, u32[]{:S(2)}) copy-start(f32[96,768]{1,0:T(8,128)} %am.1) | copy-start | bytes 884740
  221.5 5.5 %copy-start.10 = (f32[96,768]{1,0:T(8,128)S(1)}, f32[96,768]{1,0:T(8,128)}, u32[]{:S(2)}) copy-start(f32[96,768]{1,0:T(8,128)} %param.19) | copy-start | bytes 884740
  221.5 5.5 %copy-start.11 = (f32[96,768]{1,0:T(8,128)S(1)}, f32[96,768]{1,0:T(8,128)}, u32[]{:S(2)}) copy-start(f32[96,768]{1,0:T(8,128)} %param.20) | copy-start | bytes 884740
  221.6 5.5 %copy-start.12 = (f32[96,768]{1,0:T(8,128)S(1)}, f32[96,768]{1,0:T(8,128)}, u32[]{:S(2)}) copy-start(f32[96,768]{1,0:T(8,128)} %get-tuple-element.42) | copy-start | bytes 884740
  221.6 6.6 %copy-start.9 = (f32[96,768]{1,0:T(8,128)S(1)}, f32[96,768]{1,0:T(8,128)}, u32[]{:S(2)}) copy-start(f32[96,768]{1,0:T(8,128)} %get-tuple-element.44) | copy-start | bytes 884740
  227.0 1.1 copy-start.1
  227.0 1.1 copy-start.2
  227.0 1.3 copy-start.4
  227.0 1.5 copy-start.5
  227.0 1.6 copy-start.6
  227.0 1.7 copy-start.7
  227.0 1.8 copy-start.8
  228.8 1.5 copy-start.14
  228.8 1.5 copy-start.15
